TPU v7x, 32 devices: a whole 2x2x4 slice. The times are simulated.
32 devices in a mesh: narrow: 4 (over z), wide: 8 (over y, x, core).
Axes of the slice: x: 2, y: 2, z: 4, core: 2. Of those that a mesh axis runs over, the one named last changes fastest.
Arguments:
- tokens: bfloat16 [12288, 640], P('wide'), may hold values from -6 to 6
- cotangent: bfloat16 [12288, 640], P('wide'), may hold values from -6 to 6
- seq_lens: int32 [8, 16], P('wide'), may hold values from 1 to 1024, 1536 in all within a row
- norm_gains: bfloat16 [2, 640], replicated, may hold values from 0.099609375 to 1.8984375
- norm_shifts: bfloat16 [2, 640], replicated, may hold values from -3 to 3
- w_qkv: bfloat16 [3, 640, 640], P(None, 'wide', 'narrow'), may hold values from -0.25 to 0.25
- w_attn_out: bfloat16 [640, 640], P('narrow', 'wide'), may hold values from -2 to 2
- w_ffn_in: bfloat16 [640, 5120], P('narrow', 'wide'), may hold values from -0.25 to 0.25
- w_ffn_down: bfloat16 [640, 5120], P('narrow', 'wide'), may hold values from -0.078125 to 0.078125
Outputs:
- layer_out: bfloat16 [12288, 640], P('wide')
- input_grad: bfloat16 [12288, 640], P('wide')
- grad_norm_gains: float32 [2, 640], P(None, 'wide')
- grad_norm_shifts: float32 [2, 640], P(None, 'wide')
- grad_qkv: float32 [3, 640, 640], P(None, 'wide', 'narrow')
- grad_attn_out: float32 [640, 640], P('narrow', 'wide')
- grad_ffn_in: float32 [640, 5120], P('narrow', 'wide')
- grad_ffn_down: float32 [640, 5120], P('narrow', 'wide')
Inputs may be any that keep to these rules, and one draw needn't show every extreme that they name: `seq_lens`: each row lists the lengths of the 16 sequences packed end to end in that index's 1536 slots; a row sums to 1536 and its largest entry is exactly 1024.
All inputs are finite; a program needn't handle non-finite values.
Results may differ from a plain program's by a relative error of at most 0.015.
Values may be sent and summed in bfloat16 or wider, within the bound.
No kernel may reach another device: no remote copies, remote signals or barrier semaphores. Data moves between devices by JAX's collectives and lax.ppermute only.
A program may use at most 128 MiB of HBM per device.

v0:
```python
from functools import partial
import jax
import jax.numpy as jnp
from jax import lax
from jax.sharding import PartitionSpec as P

HD = 32
QBLK = 512
FBLK = 128
EPS = 1e-05


def layer_norm(rows, gain, shift):
    center = rows - jnp.mean(rows, axis=-1, keepdims=True)
    spread = jnp.mean(center * center, axis=-1, keepdims=True)
    return center * lax.rsqrt(spread + EPS) * gain + shift


def segment_ids(lengths, count):
    ends = jnp.cumsum(lengths, dtype=jnp.int32)
    position = jnp.arange(count, dtype=jnp.int32)
    return jnp.sum((position[:, None] >= ends[None, :]).astype(jnp.int32), axis=1)


def block_scores(q_block, keys, seg_block, segment):
    scores = jnp.einsum("qd,kd->qk", q_block, keys, preferred_element_type=jnp.float32) * HD ** (
        -0.5
    )
    return jnp.where(seg_block[:, None] == segment[None, :], scores, -1e30)


def attend_forward(query, key, value, segment):
    count, width = query.shape
    starts = jnp.arange(count // QBLK, dtype=jnp.int32) * QBLK

    def one_head(head):
        q_head = lax.dynamic_slice_in_dim(query, head * HD, HD, 1)
        k_head = lax.dynamic_slice_in_dim(key, head * HD, HD, 1)
        v_head = lax.dynamic_slice_in_dim(value, head * HD, HD, 1)

        def one_block(start):
            q_block = lax.dynamic_slice_in_dim(q_head, start, QBLK, 0)
            seg_block = lax.dynamic_slice_in_dim(segment, start, QBLK, 0)
            scores = block_scores(q_block, k_head, seg_block, segment)
            top = jnp.max(scores, axis=1, keepdims=True)
            expd = jnp.exp(scores - top)
            total = jnp.sum(expd, axis=1, keepdims=True)
            weights = (expd / total).astype(jnp.bfloat16)
            result = jnp.dot(weights, v_head, preferred_element_type=jnp.float32)
            return (result, (top + jnp.log(total))[:, 0])

        results, logsum = lax.map(one_block, starts)
        return (results.reshape(count, HD), logsum.reshape(count))

    results, logsum = lax.map(one_head, jnp.arange(width // HD, dtype=jnp.int32))
    return (results.transpose(1, 0, 2).reshape(count, width), logsum)


def attend_backward(query, key, value, dattended, logsum, segment):
    count, width = query.shape
    starts = jnp.arange(count // QBLK, dtype=jnp.int32) * QBLK
    scale = HD ** (-0.5)

    def one_head(head):
        q_head = lax.dynamic_slice_in_dim(query, head * HD, HD, 1)
        k_head = lax.dynamic_slice_in_dim(key, head * HD, HD, 1)
        v_head = lax.dynamic_slice_in_dim(value, head * HD, HD, 1)
        d_head = lax.dynamic_slice_in_dim(dattended, head * HD, HD, 1)
        log_head = logsum[head]

        def one_block(carry, start):
            dkey, dvalue = carry
            q_block = lax.dynamic_slice_in_dim(q_head, start, QBLK, 0)
            d_block = lax.dynamic_slice_in_dim(d_head, start, QBLK, 0)
            seg_block = lax.dynamic_slice_in_dim(segment, start, QBLK, 0)
            log_block = lax.dynamic_slice_in_dim(log_head, start, QBLK, 0)
            scores = block_scores(q_block, k_head, seg_block, segment)
            prob = jnp.exp(scores - log_block[:, None])
            dprob = jnp.einsum("qd,kd->qk", d_block, v_head, preferred_element_type=jnp.float32)
            delta = jnp.sum(prob * dprob, axis=1, keepdims=True)
            dscore = (prob * (dprob - delta)).astype(jnp.bfloat16)
            dquery = jnp.dot(dscore, k_head, preferred_element_type=jnp.float32) * scale
            dkey = (
                dkey
                + jnp.einsum("qk,qd->kd", dscore, q_block, preferred_element_type=jnp.float32)
                * scale
            )
            dvalue = dvalue + jnp.einsum(
                "qk,qd->kd", prob.astype(jnp.bfloat16), d_block, preferred_element_type=jnp.float32
            )
            return ((dkey, dvalue), dquery)

        zeros = jnp.zeros((count, HD), jnp.float32)
        (dkey, dvalue), dquery = lax.scan(one_block, (zeros, zeros), starts)
        return (dquery.reshape(count, HD), dkey, dvalue)

    dquery, dkey, dvalue = lax.map(one_head, jnp.arange(width // HD, dtype=jnp.int32))

    def joined(arr):
        return arr.transpose(1, 0, 2).reshape(count, width)

    return (joined(dquery), joined(dkey), joined(dvalue))


def hidden_block(normed_mine, ffn_in_full, start):
    x_block = lax.dynamic_slice_in_dim(normed_mine, start, FBLK, 0)
    share = lax.psum_scatter(
        jnp.dot(x_block, ffn_in_full, preferred_element_type=jnp.float32),
        "narrow",
        scatter_dimension=0,
        tiled=True,
    )
    act_share = jax.nn.gelu(share, approximate=False).astype(jnp.bfloat16)
    act_rows = lax.all_gather(act_share, "narrow", axis=0, tiled=True)
    return (x_block, share, act_rows)


def local(
    tokens, cotangent, seq_lens, norm_gains, norm_shifts, w_qkv, w_attn_out, w_ffn_in, w_ffn_down
):
    count = tokens.shape[0]
    width = w_attn_out.shape[0]
    first_col = lax.axis_index("narrow") * width
    gains = norm_gains.astype(jnp.float32)
    shifts = norm_shifts.astype(jnp.float32)
    segment = segment_ids(seq_lens[0], count)
    resid = tokens.astype(jnp.float32)
    dy_full = cotangent.astype(jnp.float32)
    qkv_full, out_full = (
        lax.all_gather(w_qkv, "wide", axis=1, tiled=True),
        lax.all_gather(w_attn_out, "wide", axis=1, tiled=True),
    )
    normed_low = layer_norm(resid, gains[0], shifts[0]).astype(jnp.bfloat16)
    proj = jnp.einsum(
        "td,jde->jte", normed_low, qkv_full, preferred_element_type=jnp.float32
    ).astype(jnp.bfloat16)
    query, key, value = (proj[0], proj[1], proj[2])
    attended, logsum = attend_forward(query, key, value, segment)
    attended_low = attended.astype(jnp.bfloat16)
    mixed = jnp.dot(attended_low, out_full, preferred_element_type=jnp.float32)
    mixed_mine = lax.psum_scatter(mixed, "narrow", scatter_dimension=1, tiled=True)
    middle_mine = lax.dynamic_slice_in_dim(resid, first_col, width, 1) + mixed_mine
    middle = lax.all_gather(middle_mine, "narrow", axis=1, tiled=True)
    normed_two = layer_norm(middle, gains[1], shifts[1])
    ffn_in_part, ffn_down_part = (
        lax.all_gather(w_ffn_in, "wide", axis=1, tiled=True),
        lax.all_gather(w_ffn_down, "wide", axis=1, tiled=True),
    )
    dy_cols = lax.dynamic_slice_in_dim(cotangent, first_col, width, 1)
    normed_mine = lax.dynamic_slice_in_dim(normed_two, first_col, width, 1).astype(jnp.bfloat16)
    starts = jnp.arange(count // FBLK, dtype=jnp.int32) * FBLK

    def ffn_forward(carry, start):
        x_block, share, act_rows = hidden_block(normed_mine, ffn_in_part, start)
        result = lax.dot_general(
            act_rows, ffn_down_part, (((1,), (1,)), ((), ())), preferred_element_type=jnp.float32
        )
        return (carry, result)

    _, branch = lax.scan(ffn_forward, jnp.zeros((), jnp.float32), starts)
    branch_full = lax.all_gather(
        branch.reshape(count, width).astype(jnp.bfloat16), "narrow", axis=1, tiled=True
    ).astype(jnp.float32)
    layer_out = (middle + branch_full).astype(jnp.bfloat16)

    def ffn_backward(carry, start):
        grad_in, grad_down = carry
        x_block, share, act_rows = hidden_block(normed_mine, ffn_in_part, start)
        dy_block = lax.dynamic_slice_in_dim(dy_cols, start, FBLK, 0)
        dact = lax.psum_scatter(
            jnp.dot(dy_block, ffn_down_part, preferred_element_type=jnp.float32),
            "narrow",
            scatter_dimension=0,
            tiled=True,
        )
        _, gelu_back = jax.vjp(partial(jax.nn.gelu, approximate=False), share)
        dshare = gelu_back(dact)[0].astype(jnp.bfloat16)
        drows = lax.all_gather(dshare, "narrow", axis=0, tiled=True)
        grad_in = grad_in + lax.dot_general(
            x_block, drows, (((0,), (0,)), ((), ())), preferred_element_type=jnp.float32
        )
        grad_down = grad_down + lax.dot_general(
            dy_block, act_rows, (((0,), (0,)), ((), ())), preferred_element_type=jnp.float32
        )
        dnormed = lax.dot_general(
            drows, ffn_in_part, (((1,), (1,)), ((), ())), preferred_element_type=jnp.float32
        )
        return ((grad_in, grad_down), dnormed)

    empty = jnp.zeros(ffn_in_part.shape, jnp.float32)
    (grad_in, grad_down), dnormed = lax.scan(ffn_backward, (empty, empty), starts)
    dnormed_two = lax.all_gather(dnormed.reshape(count, width), "narrow", axis=1, tiled=True)
    grad_in_out, grad_down_out = (
        lax.psum_scatter(grad_in, "wide", scatter_dimension=1, tiled=True),
        lax.psum_scatter(grad_down, "wide", scatter_dimension=1, tiled=True),
    )
    _, norm_back_two = jax.vjp(layer_norm, middle, gains[1], shifts[1])
    dmiddle, dgain_two, dshift_two = norm_back_two(dnormed_two)
    dmiddle = dmiddle + dy_full
    dmixed_low = dmiddle.astype(jnp.bfloat16)
    grad_out = lax.dot_general(
        attended_low, dmixed_low, (((0,), (0,)), ((), ())), preferred_element_type=jnp.float32
    )
    dattended = lax.dot_general(
        dmixed_low, out_full, (((1,), (1,)), ((), ())), preferred_element_type=jnp.float32
    ).astype(jnp.bfloat16)
    dquery, dkey, dvalue = attend_backward(query, key, value, dattended, logsum, segment)
    dproj = jnp.stack([dquery, dkey, dvalue]).astype(jnp.bfloat16)
    grad_proj = jnp.einsum("td,jte->jde", normed_low, dproj, preferred_element_type=jnp.float32)
    dnormed_part = jnp.einsum("jte,jde->td", dproj, qkv_full, preferred_element_type=jnp.float32)
    dnormed_one = lax.psum(dnormed_part.astype(jnp.bfloat16), "narrow").astype(jnp.float32)
    _, norm_back_one = jax.vjp(layer_norm, resid, gains[0], shifts[0])
    dresid, dgain_one, dshift_one = norm_back_one(dnormed_one)
    input_grad = (dmiddle + dresid).astype(jnp.bfloat16)
    dgains = jnp.stack([dgain_one, dgain_two])
    dshifts = jnp.stack([dshift_one, dshift_two])
    gain_out, shift_out, proj_out, attn_out = (
        lax.psum_scatter(dgains, "wide", scatter_dimension=1, tiled=True),
        lax.psum_scatter(dshifts, "wide", scatter_dimension=1, tiled=True),
        lax.psum_scatter(grad_proj, "wide", scatter_dimension=1, tiled=True),
        lax.psum_scatter(grad_out, "wide", scatter_dimension=1, tiled=True),
    )
    return (
        layer_out,
        input_grad,
        gain_out,
        shift_out,
        proj_out,
        attn_out,
        grad_in_out,
        grad_down_out,
    )


def solution(mesh):
    placed = (
        P("wide", None),
        P("wide", None),
        P("wide", None),
        P(),
        P(),
        P(None, "wide", "narrow"),
        P("narrow", "wide"),
        P("narrow", "wide"),
        P("narrow", "wide"),
    )
    return jax.shard_map(
        local,
        mesh=mesh,
        in_specs=placed,
        out_specs=(
            P("wide", None),
            P("wide", None),
            P(None, "wide"),
            P(None, "wide"),
            P(None, "wide", "narrow"),
            P("narrow", "wide"),
            P("narrow", "wide"),
            P("narrow", "wide"),
        ),
        check_vma=False,
    )
```

profile of v0, /device:TPU:0, one launch (start us, length us, event | category | flops | bytes accessed | tf_op | source)
XLA Modules:
  0.0 4609.1 jit_solution(13928919483076880924)
XLA Ops:
  36.1 182.4 %while.84 = (s32[]{:T(128)}, bf16[5,1536,32]{1,2,0:T(8,128)(2,1)}, f32[5,1536]{1,0:T(8,128)}, s32[5]{0:T(128)}, bf16[1536,160]{1,0:T(8,128)(2,1)}, /*index=5*/bf...) while((s32[]{:T(128)}, bf16[5,1536,32]{1,2,0:T(8,128)(2,1)}, ...), condition=%wide.region_9.10_spmd.clone, body=%wide.region_4.9_spmd.clone.sunk | while | flops 107740680 | bytes 11363814 | solution.py:55
  236.6 69.2 %reduce-scatter.19.cloned.1.call-done = f32[1536,160]{0,1:T(8,128)} async-done(((f32[1536,640]{0,1:T(8,128)}), f32[1536,160]{0,1:T(8,128)}) %reduce-scatter.19.cloned.1.call-update) | async-done | bytes 983056 | tf_op jit(solution)/shard_map/reduce_scatter | solution.py:141
  312.1 73.2 %all-gather.9.cloned.1.call-done = f32[1536,640]{0,1:T(8,128)} async-done(((f32[1536,160]{0,1:T(8,128)}), f32[1536,640]{0,1:T(8,128)}) %all-gather.9.cloned.1.call-update) | async-done | bytes 3932176 | tf_op jit(solution)/shard_map/all_gather | solution.py:143
  439.6 2218.3 %while.87 = (s32[]{:T(128)}, f32[160,5120]{1,0:T(8,128)}, f32[160,5120]{1,0:T(8,128)}, f32[12,128,160]{1,0,2:T(8,128)}, s32[12]{0:T(128)S(1)}, /*index=5*/bf16[1...) while((s32[]{:T(128)}, f32[160,5120]{1,0:T(8,128)}, ...), condition=%wide.region_19.20_spmd.clone, body=%wide.region_16.19_spmd.clone.sunk | while | flops 1064796160 | bytes 83411448 | solution.py:191
  448.0 50.1 %reduce-scatter.37.cloned.1.call-done = f32[32,5120]{1,0:T(8,128)} async-done(((f32[128,5120]{1,0:T(8,128)}), f32[32,5120]{1,0:T(8,128)}) %reduce-scatter.37.cloned.1.call-update) | async-done | bytes 655376 | tf_op jit(solution)/shard_map/while/body/eval_jaxpr/reduce_scatter | solution.py:107
  501.3 50.8 %reduce-scatter.35.cloned.1.call-done = f32[32,5120]{1,0:T(8,128)} async-done(((f32[128,5120]{1,0:T(8,128)}), f32[32,5120]{1,0:T(8,128)}) %reduce-scatter.35.cloned.1.call-update) | async-done | bytes 655376 | tf_op jit(solution)/shard_map/while/body/eval_jaxpr/reduce_scatter | solution.py:170
  632.9 49.1 %reduce-scatter.37.cloned.1.call-done = f32[32,5120]{1,0:T(8,128)} async-done(((f32[128,5120]{1,0:T(8,128)}), f32[32,5120]{1,0:T(8,128)}) %reduce-scatter.37.cloned.1.call-update) | async-done | bytes 655376 | tf_op jit(solution)/shard_map/while/body/eval_jaxpr/reduce_scatter | solution.py:107
  685.1 50.8 %reduce-scatter.35.cloned.1.call-done = f32[32,5120]{1,0:T(8,128)} async-done(((f32[128,5120]{1,0:T(8,128)}), f32[32,5120]{1,0:T(8,128)}) %reduce-scatter.35.cloned.1.call-update) | async-done | bytes 655376 | tf_op jit(solution)/shard_map/while/body/eval_jaxpr/reduce_scatter | solution.py:170
  817.6 49.1 %reduce-scatter.37.cloned.1.call-done = f32[32,5120]{1,0:T(8,128)} async-done(((f32[128,5120]{1,0:T(8,128)}), f32[32,5120]{1,0:T(8,128)}) %reduce-scatter.37.cloned.1.call-update) | async-done | bytes 655376 | tf_op jit(solution)/shard_map/while/body/eval_jaxpr/reduce_scatter | solution.py:107
  869.9 50.8 %reduce-scatter.35.cloned.1.call-done = f32[32,5120]{1,0:T(8,128)} async-done(((f32[128,5120]{1,0:T(8,128)}), f32[32,5120]{1,0:T(8,128)}) %reduce-scatter.35.cloned.1.call-update) | async-done | bytes 655376 | tf_op jit(solution)/shard_map/while/body/eval_jaxpr/reduce_scatter | solution.py:170
  1002.3 49.1 %reduce-scatter.37.cloned.1.call-done = f32[32,5120]{1,0:T(8,128)} async-done(((f32[128,5120]{1,0:T(8,128)}), f32[32,5120]{1,0:T(8,128)}) %reduce-scatter.37.cloned.1.call-update) | async-done | bytes 655376 | tf_op jit(solution)/shard_map/while/body/eval_jaxpr/reduce_scatter | solution.py:107
  1054.6 50.8 %reduce-scatter.35.cloned.1.call-done = f32[32,5120]{1,0:T(8,128)} async-done(((f32[128,5120]{1,0:T(8,128)}), f32[32,5120]{1,0:T(8,128)}) %reduce-scatter.35.cloned.1.call-update) | async-done | bytes 655376 | tf_op jit(solution)/shard_map/while/body/eval_jaxpr/reduce_scatter | solution.py:170
  1187.0 49.1 %reduce-scatter.37.cloned.1.call-done = f32[32,5120]{1,0:T(8,128)} async-done(((f32[128,5120]{1,0:T(8,128)}), f32[32,5120]{1,0:T(8,128)}) %reduce-scatter.37.cloned.1.call-update) | async-done | bytes 655376 | tf_op jit(solution)/shard_map/while/body/eval_jaxpr/reduce_scatter | solution.py:107
  1239.3 50.9 %reduce-scatter.35.cloned.1.call-done = f32[32,5120]{1,0:T(8,128)} async-done(((f32[128,5120]{1,0:T(8,128)}), f32[32,5120]{1,0:T(8,128)}) %reduce-scatter.35.cloned.1.call-update) | async-done | bytes 655376 | tf_op jit(solution)/shard_map/while/body/eval_jaxpr/reduce_scatter | solution.py:170
  1371.9 49.1 %reduce-scatter.37.cloned.1.call-done = f32[32,5120]{1,0:T(8,128)} async-done(((f32[128,5120]{1,0:T(8,128)}), f32[32,5120]{1,0:T(8,128)}) %reduce-scatter.37.cloned.1.call-update) | async-done | bytes 655376 | tf_op jit(solution)/shard_map/while/body/eval_jaxpr/reduce_scatter | solution.py:107
  1424.2 50.8 %reduce-scatter.35.cloned.1.call-done = f32[32,5120]{1,0:T(8,128)} async-done(((f32[128,5120]{1,0:T(8,128)}), f32[32,5120]{1,0:T(8,128)}) %reduce-scatter.35.cloned.1.call-update) | async-done | bytes 655376 | tf_op jit(solution)/shard_map/while/body/eval_jaxpr/reduce_scatter | solution.py:170
  1556.8 49.1 %reduce-scatter.37.cloned.1.call-done = f32[32,5120]{1,0:T(8,128)} async-done(((f32[128,5120]{1,0:T(8,128)}), f32[32,5120]{1,0:T(8,128)}) %reduce-scatter.37.cloned.1.call-update) | async-done | bytes 655376 | tf_op jit(solution)/shard_map/while/body/eval_jaxpr/reduce_scatter | solution.py:107
  1609.1 50.8 %reduce-scatter.35.cloned.1.call-done = f32[32,5120]{1,0:T(8,128)} async-done(((f32[128,5120]{1,0:T(8,128)}), f32[32,5120]{1,0:T(8,128)}) %reduce-scatter.35.cloned.1.call-update) | async-done | bytes 655376 | tf_op jit(solution)/shard_map/while/body/eval_jaxpr/reduce_scatter | solution.py:170
  1741.7 49.1 %reduce-scatter.37.cloned.1.call-done = f32[32,5120]{1,0:T(8,128)} async-done(((f32[128,5120]{1,0:T(8,128)}), f32[32,5120]{1,0:T(8,128)}) %reduce-scatter.37.cloned.1.call-update) | async-done | bytes 655376 | tf_op jit(solution)/shard_map/while/body/eval_jaxpr/reduce_scatter | solution.py:107
  1794.0 50.9 %reduce-scatter.35.cloned.1.call-done = f32[32,5120]{1,0:T(8,128)} async-done(((f32[128,5120]{1,0:T(8,128)}), f32[32,5120]{1,0:T(8,128)}) %reduce-scatter.35.cloned.1.call-update) | async-done | bytes 655376 | tf_op jit(solution)/shard_map/while/body/eval_jaxpr/reduce_scatter | solution.py:170
  1926.5 49.1 %reduce-scatter.37.cloned.1.call-done = f32[32,5120]{1,0:T(8,128)} async-done(((f32[128,5120]{1,0:T(8,128)}), f32[32,5120]{1,0:T(8,128)}) %reduce-scatter.37.cloned.1.call-update) | async-done | bytes 655376 | tf_op jit(solution)/shard_map/while/body/eval_jaxpr/reduce_scatter | solution.py:107
  1978.8 50.9 %reduce-scatter.35.cloned.1.call-done = f32[32,5120]{1,0:T(8,128)} async-done(((f32[128,5120]{1,0:T(8,128)}), f32[32,5120]{1,0:T(8,128)}) %reduce-scatter.35.cloned.1.call-update) | async-done | bytes 655376 | tf_op jit(solution)/shard_map/while/body/eval_jaxpr/reduce_scatter | solution.py:170
  2111.5 49.1 %reduce-scatter.37.cloned.1.call-done = f32[32,5120]{1,0:T(8,128)} async-done(((f32[128,5120]{1,0:T(8,128)}), f32[32,5120]{1,0:T(8,128)}) %reduce-scatter.37.cloned.1.call-update) | async-done | bytes 655376 | tf_op jit(solution)/shard_map/while/body/eval_jaxpr/reduce_scatter | solution.py:107
  2163.8 50.9 %reduce-scatter.35.cloned.1.call-done = f32[32,5120]{1,0:T(8,128)} async-done(((f32[128,5120]{1,0:T(8,128)}), f32[32,5120]{1,0:T(8,128)}) %reduce-scatter.35.cloned.1.call-update) | async-done | bytes 655376 | tf_op jit(solution)/shard_map/while/body/eval_jaxpr/reduce_scatter | solution.py:170
  2296.6 49.1 %reduce-scatter.37.cloned.1.call-done = f32[32,5120]{1,0:T(8,128)} async-done(((f32[128,5120]{1,0:T(8,128)}), f32[32,5120]{1,0:T(8,128)}) %reduce-scatter.37.cloned.1.call-update) | async-done | bytes 655376 | tf_op jit(solution)/shard_map/while/body/eval_jaxpr/reduce_scatter | solution.py:107
  2348.9 50.8 %reduce-scatter.35.cloned.1.call-done = f32[32,5120]{1,0:T(8,128)} async-done(((f32[128,5120]{1,0:T(8,128)}), f32[32,5120]{1,0:T(8,128)}) %reduce-scatter.35.cloned.1.call-update) | async-done | bytes 655376 | tf_op jit(solution)/shard_map/while/body/eval_jaxpr/reduce_scatter | solution.py:170
  2481.3 49.1 %reduce-scatter.37.cloned.1.call-done = f32[32,5120]{1,0:T(8,128)} async-done(((f32[128,5120]{1,0:T(8,128)}), f32[32,5120]{1,0:T(8,128)}) %reduce-scatter.37.cloned.1.call-update) | async-done | bytes 655376 | tf_op jit(solution)/shard_map/while/body/eval_jaxpr/reduce_scatter | solution.py:107
  2533.6 50.9 %reduce-scatter.35.cloned.1.call-done = f32[32,5120]{1,0:T(8,128)} async-done(((f32[128,5120]{1,0:T(8,128)}), f32[32,5120]{1,0:T(8,128)}) %reduce-scatter.35.cloned.1.call-update) | async-done | bytes 655376 | tf_op jit(solution)/shard_map/while/body/eval_jaxpr/reduce_scatter | solution.py:170
  2660.5 1148.4 %while.82 = (s32[]{:T(128)}, bf16[12,128,160]{1,2,0:T(8,128)(2,1)}, s32[12]{0:T(128)S(1)}, bf16[1536,160]{1,0:T(8,128)(2,1)}, bf16[160,5120]{1,0:T(8,128)(2,1)},...) while((s32[]{:T(128)}, bf16[12,128,160]{1,2,0:T(8,128)(2,1)}, s32[12]{0:T(128)S(1)}, ...), condition=%wide.region_15.16_spmd, body=%wide.region_13.15_spmd.sunk | while | flops 430080000 | bytes 29638920 | solution.py:160
  2666.7 51.2 %reduce-scatter.33.cloned.1.call-done = f32[32,5120]{1,0:T(8,128)} async-done(((f32[128,5120]{1,0:T(8,128)}), f32[32,5120]{1,0:T(8,128)}) %reduce-scatter.33.cloned.1.call-update) | async-done | bytes 655376 | tf_op jit(solution)/shard_map/while/body/eval_jaxpr/reduce_scatter | solution.py:107
  2762.4 51.2 %reduce-scatter.33.cloned.1.call-done = f32[32,5120]{1,0:T(8,128)} async-done(((f32[128,5120]{1,0:T(8,128)}), f32[32,5120]{1,0:T(8,128)}) %reduce-scatter.33.cloned.1.call-update) | async-done | bytes 655376 | tf_op jit(solution)/shard_map/while/body/eval_jaxpr/reduce_scatter | solution.py:107
  2816.9 32.6 all-gather.19.cloned.1.call-done
  2858.2 51.2 %reduce-scatter.33.cloned.1.call-done = f32[32,5120]{1,0:T(8,128)} async-done(((f32[128,5120]{1,0:T(8,128)}), f32[32,5120]{1,0:T(8,128)}) %reduce-scatter.33.cloned.1.call-update) | async-done | bytes 655376 | tf_op jit(solution)/shard_map/while/body/eval_jaxpr/reduce_scatter | solution.py:107
  2912.6 32.5 all-gather.19.cloned.1.call-done
  2953.9 51.2 %reduce-scatter.33.cloned.1.call-done = f32[32,5120]{1,0:T(8,128)} async-done(((f32[128,5120]{1,0:T(8,128)}), f32[32,5120]{1,0:T(8,128)}) %reduce-scatter.33.cloned.1.call-update) | async-done | bytes 655376 | tf_op jit(solution)/shard_map/while/body/eval_jaxpr/reduce_scatter | solution.py:107
  3008.3 32.5 all-gather.19.cloned.1.call-done
  3049.6 51.2 %reduce-scatter.33.cloned.1.call-done = f32[32,5120]{1,0:T(8,128)} async-done(((f32[128,5120]{1,0:T(8,128)}), f32[32,5120]{1,0:T(8,128)}) %reduce-scatter.33.cloned.1.call-update) | async-done | bytes 655376 | tf_op jit(solution)/shard_map/while/body/eval_jaxpr/reduce_scatter | solution.py:107
  3104.0 32.5 all-gather.19.cloned.1.call-done
  3145.3 51.2 %reduce-scatter.33.cloned.1.call-done = f32[32,5120]{1,0:T(8,128)} async-done(((f32[128,5120]{1,0:T(8,128)}), f32[32,5120]{1,0:T(8,128)}) %reduce-scatter.33.cloned.1.call-update) | async-done | bytes 655376 | tf_op jit(solution)/shard_map/while/body/eval_jaxpr/reduce_scatter | solution.py:107
  3199.7 32.5 all-gather.19.cloned.1.call-done
  3241.0 51.2 %reduce-scatter.33.cloned.1.call-done = f32[32,5120]{1,0:T(8,128)} async-done(((f32[128,5120]{1,0:T(8,128)}), f32[32,5120]{1,0:T(8,128)}) %reduce-scatter.33.cloned.1.call-update) | async-done | bytes 655376 | tf_op jit(solution)/shard_map/while/body/eval_jaxpr/reduce_scatter | solution.py:107
  3295.4 32.6 all-gather.19.cloned.1.call-done
  3336.7 51.2 %reduce-scatter.33.cloned.1.call-done = f32[32,5120]{1,0:T(8,128)} async-done(((f32[128,5120]{1,0:T(8,128)}), f32[32,5120]{1,0:T(8,128)}) %reduce-scatter.33.cloned.1.call-update) | async-done | bytes 655376 | tf_op jit(solution)/shard_map/while/body/eval_jaxpr/reduce_scatter | solution.py:107
  3391.1 32.5 all-gather.19.cloned.1.call-done
  3432.4 51.2 %reduce-scatter.33.cloned.1.call-done = f32[32,5120]{1,0:T(8,128)} async-done(((f32[128,5120]{1,0:T(8,128)}), f32[32,5120]{1,0:T(8,128)}) %reduce-scatter.33.cloned.1.call-update) | async-done | bytes 655376 | tf_op jit(solution)/shard_map/while/body/eval_jaxpr/reduce_scatter | solution.py:107
  3486.8 32.5 all-gather.19.cloned.1.call-done
  3528.1 51.2 %reduce-scatter.33.cloned.1.call-done = f32[32,5120]{1,0:T(8,128)} async-done(((f32[128,5120]{1,0:T(8,128)}), f32[32,5120]{1,0:T(8,128)}) %reduce-scatter.33.cloned.1.call-update) | async-done | bytes 655376 | tf_op jit(solution)/shard_map/while/body/eval_jaxpr/reduce_scatter | solution.py:107
  3582.5 32.5 all-gather.19.cloned.1.call-done
  3623.8 51.2 %reduce-scatter.33.cloned.1.call-done = f32[32,5120]{1,0:T(8,128)} async-done(((f32[128,5120]{1,0:T(8,128)}), f32[32,5120]{1,0:T(8,128)}) %reduce-scatter.33.cloned.1.call-update) | async-done | bytes 655376 | tf_op jit(solution)/shard_map/while/body/eval_jaxpr/reduce_scatter | solution.py:107
  3719.5 51.2 %reduce-scatter.33.cloned.1.call-done = f32[32,5120]{1,0:T(8,128)} async-done(((f32[128,5120]{1,0:T(8,128)}), f32[32,5120]{1,0:T(8,128)}) %reduce-scatter.33.cloned.1.call-update) | async-done | bytes 655376 | tf_op jit(solution)/shard_map/while/body/eval_jaxpr/reduce_scatter | solution.py:107
  3773.9 32.5 all-gather.19.cloned.1.call-done
  3814.6 72.3 %all-gather.17.cloned.1.call-done = f32[1536,640]{0,1:T(8,128)} async-done(((f32[1536,160]{0,1:T(8,128)}), f32[1536,640]{0,1:T(8,128)}) %all-gather.17.cloned.1.call-update) | async-done | bytes 3932176 | tf_op jit(solution)/shard_map/all_gather | solution.py:192
  3892.1 38.5 all-gather.15.cloned.1.call-done
  3942.7 319.0 %while.86 = (s32[]{:T(128)}, bf16[5,1536,32]{2,1,0:T(8,128)(2,1)}, bf16[5,1536,32]{1,2,0:T(8,128)(2,1)}, bf16[5,1536,32]{1,2,0:T(8,128)(2,1)}, s32[5]{0:T(128)},...) while((s32[]{:T(128)}, bf16[5,1536,32]{2,1,0:T(8,128)(2,1)}, ...), condition=%wide.region_26.27_spmd.clone, body=%wide.region_22.26_spmd.clone.sunk | while | flops 259784208 | bytes 27660404 | solution.py:97
  3954.5 48.4 %while.89 = (s32[]{:T(128)}, f32[1536,32]{0,1:T(8,128)}, f32[1536,32]{0,1:T(8,128)}, bf16[3,512,32]{1,2,0:T(8,128)(2,1)}, s32[3]{0:T(128)}, /*index=5*/s32[1536]...) while((s32[]{:T(128)}, f32[1536,32]{0,1:T(8,128)}, ...), condition=%wide.region_25.25_spmd.clone, body=%wide.region_23.24_spmd.clone.sunk | while | flops 259784192 | bytes 25385684 | solution.py:94
  4018.4 48.4 %while.89 = (s32[]{:T(128)}, f32[1536,32]{0,1:T(8,128)}, f32[1536,32]{0,1:T(8,128)}, bf16[3,512,32]{1,2,0:T(8,128)(2,1)}, s32[3]{0:T(128)}, /*index=5*/s32[1536]...) while((s32[]{:T(128)}, f32[1536,32]{0,1:T(8,128)}, ...), condition=%wide.region_25.25_spmd.clone, body=%wide.region_23.24_spmd.clone.sunk | while | flops 259784192 | bytes 25385684 | solution.py:94
  4082.2 48.4 %while.89 = (s32[]{:T(128)}, f32[1536,32]{0,1:T(8,128)}, f32[1536,32]{0,1:T(8,128)}, bf16[3,512,32]{1,2,0:T(8,128)(2,1)}, s32[3]{0:T(128)}, /*index=5*/s32[1536]...) while((s32[]{:T(128)}, f32[1536,32]{0,1:T(8,128)}, ...), condition=%wide.region_25.25_spmd.clone, body=%wide.region_23.24_spmd.clone.sunk | while | flops 259784192 | bytes 25385684 | solution.py:94
  4146.0 48.4 %while.89 = (s32[]{:T(128)}, f32[1536,32]{0,1:T(8,128)}, f32[1536,32]{0,1:T(8,128)}, bf16[3,512,32]{1,2,0:T(8,128)(2,1)}, s32[3]{0:T(128)}, /*index=5*/s32[1536]...) while((s32[]{:T(128)}, f32[1536,32]{0,1:T(8,128)}, ...), condition=%wide.region_25.25_spmd.clone, body=%wide.region_23.24_spmd.clone.sunk | while | flops 259784192 | bytes 25385684 | solution.py:94
  4209.8 48.4 %while.89 = (s32[]{:T(128)}, f32[1536,32]{0,1:T(8,128)}, f32[1536,32]{0,1:T(8,128)}, bf16[3,512,32]{1,2,0:T(8,128)(2,1)}, s32[3]{0:T(128)}, /*index=5*/s32[1536]...) while((s32[]{:T(128)}, f32[1536,32]{0,1:T(8,128)}, ...), condition=%wide.region_25.25_spmd.clone, body=%wide.region_23.24_spmd.clone.sunk | while | flops 259784192 | bytes 25385684 | solution.py:94
  4281.8 67.5 %all-reduce.2.cloned.1.call-done = bf16[1536,640]{0,1:T(8,128)(2,1)} async-done(((bf16[1536,640]{0,1:T(8,128)(2,1)}), bf16[1536,640]{0,1:T(8,128)(2,1)}) %all-reduce.2.cloned.1.call-update) | async-done | bytes 1966096 | tf_op jit(solution)/shard_map/psum | solution.py:211
  4387.6 39.6 reduce-scatter.29.cloned.1.call-done
  4465.3 35.4 reduce-scatter.25.cloned.1.call-done
  4502.1 49.3 %reduce-scatter.21.cloned.1.call-done = f32[160,640]{1,0:T(8,128)} async-done(((f32[160,5120]{1,0:T(8,128)}), f32[160,640]{1,0:T(8,128)}) %reduce-scatter.21.cloned.1.call-update) | async-done | bytes 409616 | tf_op jit(solution)/shard_map/reduce_scatter | solution.py:194
  4551.5 50.9 %reduce-scatter.23.cloned.1.call-done = f32[160,640]{1,0:T(8,128)} async-done(((f32[160,5120]{1,0:T(8,128)}), f32[160,640]{1,0:T(8,128)}) %reduce-scatter.23.cloned.1.call-update) | async-done | bytes 409616 | tf_op jit(solution)/shard_map/reduce_scatter | solution.py:195
  (1008 shorter events, 1969.3 us)
Async XLA Ops:
  7.2 298.6 %reduce-scatter.19.cloned.1.call-start = ((), (), s32[]{:S(2)}) async-start(), calls=%async_computation.10 | async-start | bytes 4915200 | tf_op jit(solution)/shard_map/reduce_scatter | solution.py:141
  232.6 152.7 %all-gather.9.cloned.1.call-start = ((), (), s32[]{:S(2)}) async-start(), calls=%async_computation.11 | async-start | bytes 4915200 | tf_op jit(solution)/shard_map/all_gather | solution.py:143
  308.3 103.5 %all-gather.11.cloned.1.call-start = ((), (), s32[]{:S(2)}) async-start(), calls=%async_computation.12 | async-start | bytes 1843200 | tf_op jit(solution)/shard_map/all_gather | solution.py:146
  309.1 130.5 %all-gather.13.cloned.1.call-start = ((), (), s32[]{:S(2)}) async-start(), calls=%async_computation.13 | async-start | bytes 1843200 | tf_op jit(solution)/shard_map/all_gather | solution.py:147
  439.6 58.5 %reduce-scatter.37.cloned.1.call-start = ((), (), s32[]{:S(2)}) async-start(), calls=%async_computation.26 | async-start | bytes 3276800 | tf_op jit(solution)/shard_map/while/body/eval_jaxpr/reduce_scatter | solution.py:107
  445.8 106.3 %reduce-scatter.35.cloned.1.call-start = ((), (), s32[]{:S(2)}) async-start(), calls=%async_computation.25 | async-start | bytes 3276800 | tf_op jit(solution)/shard_map/while/body/eval_jaxpr/reduce_scatter | solution.py:170
  447.9 139.0 %all-gather.21.cloned.1.call-start = ((), (), s32[]{:S(2)}) async-start(), calls=%async_computation.27 | async-start | bytes 1638400 | tf_op jit(solution)/shard_map/while/body/eval_jaxpr/all_gather | solution.py:178
  554.4 66.4 %all-gather.23.cloned.1.call-start = ((), (), s32[]{:S(2)}) async-start(), calls=%async_computation.28 | async-start | bytes 1638400 | tf_op jit(solution)/shard_map/while/body/eval_jaxpr/all_gather | solution.py:114
  630.7 105.2 %reduce-scatter.35.cloned.1.call-start = ((), (), s32[]{:S(2)}) async-start(), calls=%async_computation.25 | async-start | bytes 3276800 | tf_op jit(solution)/shard_map/while/body/eval_jaxpr/reduce_scatter | solution.py:170
  632.8 138.0 %all-gather.21.cloned.1.call-start = ((), (), s32[]{:S(2)}) async-start(), calls=%async_computation.27 | async-start | bytes 1638400 | tf_op jit(solution)/shard_map/while/body/eval_jaxpr/all_gather | solution.py:178
  738.2 66.3 %all-gather.23.cloned.1.call-start = ((), (), s32[]{:S(2)}) async-start(), calls=%async_computation.28 | async-start | bytes 1638400 | tf_op jit(solution)/shard_map/while/body/eval_jaxpr/all_gather | solution.py:114
  815.4 105.2 %reduce-scatter.35.cloned.1.call-start = ((), (), s32[]{:S(2)}) async-start(), calls=%async_computation.25 | async-start | bytes 3276800 | tf_op jit(solution)/shard_map/while/body/eval_jaxpr/reduce_scatter | solution.py:170
  817.5 138.0 %all-gather.21.cloned.1.call-start = ((), (), s32[]{:S(2)}) async-start(), calls=%async_computation.27 | async-start | bytes 1638400 | tf_op jit(solution)/shard_map/while/body/eval_jaxpr/all_gather | solution.py:178
  923.0 66.3 %all-gather.23.cloned.1.call-start = ((), (), s32[]{:S(2)}) async-start(), calls=%async_computation.28 | async-start | bytes 1638400 | tf_op jit(solution)/shard_map/while/body/eval_jaxpr/all_gather | solution.py:114
  1000.1 105.2 %reduce-scatter.35.cloned.1.call-start = ((), (), s32[]{:S(2)}) async-start(), calls=%async_computation.25 | async-start | bytes 3276800 | tf_op jit(solution)/shard_map/while/body/eval_jaxpr/reduce_scatter | solution.py:170
  1002.3 138.0 %all-gather.21.cloned.1.call-start = ((), (), s32[]{:S(2)}) async-start(), calls=%async_computation.27 | async-start | bytes 1638400 | tf_op jit(solution)/shard_map/while/body/eval_jaxpr/all_gather | solution.py:178
  1107.7 66.3 %all-gather.23.cloned.1.call-start = ((), (), s32[]{:S(2)}) async-start(), calls=%async_computation.28 | async-start | bytes 1638400 | tf_op jit(solution)/shard_map/while/body/eval_jaxpr/all_gather | solution.py:114
  1184.9 105.4 %reduce-scatter.35.cloned.1.call-start = ((), (), s32[]{:S(2)}) async-start(), calls=%async_computation.25 | async-start | bytes 3276800 | tf_op jit(solution)/shard_map/while/body/eval_jaxpr/reduce_scatter | solution.py:170
  1187.0 138.1 %all-gather.21.cloned.1.call-start = ((), (), s32[]{:S(2)}) async-start(), calls=%async_computation.27 | async-start | bytes 1638400 | tf_op jit(solution)/shard_map/while/body/eval_jaxpr/all_gather | solution.py:178
  1292.6 66.3 %all-gather.23.cloned.1.call-start = ((), (), s32[]{:S(2)}) async-start(), calls=%async_computation.28 | async-start | bytes 1638400 | tf_op jit(solution)/shard_map/while/body/eval_jaxpr/all_gather | solution.py:114
  1369.7 105.2 %reduce-scatter.35.cloned.1.call-start = ((), (), s32[]{:S(2)}) async-start(), calls=%async_computation.25 | async-start | bytes 3276800 | tf_op jit(solution)/shard_map/while/body/eval_jaxpr/reduce_scatter | solution.py:170
  1371.9 138.0 %all-gather.21.cloned.1.call-start = ((), (), s32[]{:S(2)}) async-start(), calls=%async_computation.27 | async-start | bytes 1638400 | tf_op jit(solution)/shard_map/while/body/eval_jaxpr/all_gather | solution.py:178
  1477.3 66.4 %all-gather.23.cloned.1.call-start = ((), (), s32[]{:S(2)}) async-start(), calls=%async_computation.28 | async-start | bytes 1638400 | tf_op jit(solution)/shard_map/while/body/eval_jaxpr/all_gather | solution.py:114
  1554.6 105.2 %reduce-scatter.35.cloned.1.call-start = ((), (), s32[]{:S(2)}) async-start(), calls=%async_computation.25 | async-start | bytes 3276800 | tf_op jit(solution)/shard_map/while/body/eval_jaxpr/reduce_scatter | solution.py:170
  1556.7 138.0 %all-gather.21.cloned.1.call-start = ((), (), s32[]{:S(2)}) async-start(), calls=%async_computation.27 | async-start | bytes 1638400 | tf_op jit(solution)/shard_map/while/body/eval_jaxpr/all_gather | solution.py:178
  1662.2 66.4 %all-gather.23.cloned.1.call-start = ((), (), s32[]{:S(2)}) async-start(), calls=%async_computation.28 | async-start | bytes 1638400 | tf_op jit(solution)/shard_map/while/body/eval_jaxpr/all_gather | solution.py:114
  1739.5 105.4 %reduce-scatter.35.cloned.1.call-start = ((), (), s32[]{:S(2)}) async-start(), calls=%async_computation.25 | async-start | bytes 3276800 | tf_op jit(solution)/shard_map/while/body/eval_jaxpr/reduce_scatter | solution.py:170
  1741.6 138.1 %all-gather.21.cloned.1.call-start = ((), (), s32[]{:S(2)}) async-start(), calls=%async_computation.27 | async-start | bytes 1638400 | tf_op jit(solution)/shard_map/while/body/eval_jaxpr/all_gather | solution.py:178
  1847.2 66.2 %all-gather.23.cloned.1.call-start = ((), (), s32[]{:S(2)}) async-start(), calls=%async_computation.28 | async-start | bytes 1638400 | tf_op jit(solution)/shard_map/while/body/eval_jaxpr/all_gather | solution.py:114
  1924.3 105.4 %reduce-scatter.35.cloned.1.call-start = ((), (), s32[]{:S(2)}) async-start(), calls=%async_computation.25 | async-start | bytes 3276800 | tf_op jit(solution)/shard_map/while/body/eval_jaxpr/reduce_scatter | solution.py:170
  1926.5 138.1 %all-gather.21.cloned.1.call-start = ((), (), s32[]{:S(2)}) async-start(), calls=%async_computation.27 | async-start | bytes 1638400 | tf_op jit(solution)/shard_map/while/body/eval_jaxpr/all_gather | solution.py:178
  2032.0 66.4 %all-gather.23.cloned.1.call-start = ((), (), s32[]{:S(2)}) async-start(), calls=%async_computation.28 | async-start | bytes 1638400 | tf_op jit(solution)/shard_map/while/body/eval_jaxpr/all_gather | solution.py:114
  2109.4 105.4 %reduce-scatter.35.cloned.1.call-start = ((), (), s32[]{:S(2)}) async-start(), calls=%async_computation.25 | async-start | bytes 3276800 | tf_op jit(solution)/shard_map/while/body/eval_jaxpr/reduce_scatter | solution.py:170
  2111.5 138.1 %all-gather.21.cloned.1.call-start = ((), (), s32[]{:S(2)}) async-start(), calls=%async_computation.27 | async-start | bytes 1638400 | tf_op jit(solution)/shard_map/while/body/eval_jaxpr/all_gather | solution.py:178
  2217.1 66.4 %all-gather.23.cloned.1.call-start = ((), (), s32[]{:S(2)}) async-start(), calls=%async_computation.28 | async-start | bytes 1638400 | tf_op jit(solution)/shard_map/while/body/eval_jaxpr/all_gather | solution.py:114
  2288.1 57.5 %reduce-scatter.37.cloned.1.call-start = ((), (), s32[]{:S(2)}) async-start(), calls=%async_computation.26 | async-start | bytes 3276800 | tf_op jit(solution)/shard_map/while/body/eval_jaxpr/reduce_scatter | solution.py:107
  2294.4 105.3 %reduce-scatter.35.cloned.1.call-start = ((), (), s32[]{:S(2)}) async-start(), calls=%async_computation.25 | async-start | bytes 3276800 | tf_op jit(solution)/shard_map/while/body/eval_jaxpr/reduce_scatter | solution.py:170
  2296.5 138.0 %all-gather.21.cloned.1.call-start = ((), (), s32[]{:S(2)}) async-start(), calls=%async_computation.27 | async-start | bytes 1638400 | tf_op jit(solution)/shard_map/while/body/eval_jaxpr/all_gather | solution.py:178
  2402.0 66.2 %all-gather.23.cloned.1.call-start = ((), (), s32[]{:S(2)}) async-start(), calls=%async_computation.28 | async-start | bytes 1638400 | tf_op jit(solution)/shard_map/while/body/eval_jaxpr/all_gather | solution.py:114
  2472.9 57.5 %reduce-scatter.37.cloned.1.call-start = ((), (), s32[]{:S(2)}) async-start(), calls=%async_computation.26 | async-start | bytes 3276800 | tf_op jit(solution)/shard_map/while/body/eval_jaxpr/reduce_scatter | solution.py:107
  2479.1 105.4 %reduce-scatter.35.cloned.1.call-start = ((), (), s32[]{:S(2)}) async-start(), calls=%async_computation.25 | async-start | bytes 3276800 | tf_op jit(solution)/shard_map/while/body/eval_jaxpr/reduce_scatter | solution.py:170
  2481.2 138.1 %all-gather.21.cloned.1.call-start = ((), (), s32[]{:S(2)}) async-start(), calls=%async_computation.27 | async-start | bytes 1638400 | tf_op jit(solution)/shard_map/while/body/eval_jaxpr/all_gather | solution.py:178
  2586.8 66.4 %all-gather.23.cloned.1.call-start = ((), (), s32[]{:S(2)}) async-start(), calls=%async_computation.28 | async-start | bytes 1638400 | tf_op jit(solution)/shard_map/while/body/eval_jaxpr/all_gather | solution.py:114
  2666.7 87.0 %all-gather.19.cloned.1.call-start = ((), (), s32[]{:S(2)}) async-start(), calls=%async_computation.24 | async-start | bytes 1638400 | tf_op jit(solution)/shard_map/while/body/eval_jaxpr/all_gather | solution.py:114
  2762.4 87.0 %all-gather.19.cloned.1.call-start = ((), (), s32[]{:S(2)}) async-start(), calls=%async_computation.24 | async-start | bytes 1638400 | tf_op jit(solution)/shard_map/while/body/eval_jaxpr/all_gather | solution.py:114
  2858.1 87.0 %all-gather.19.cloned.1.call-start = ((), (), s32[]{:S(2)}) async-start(), calls=%async_computation.24 | async-start | bytes 1638400 | tf_op jit(solution)/shard_map/while/body/eval_jaxpr/all_gather | solution.py:114
  2953.8 87.0 %all-gather.19.cloned.1.call-start = ((), (), s32[]{:S(2)}) async-start(), calls=%async_computation.24 | async-start | bytes 1638400 | tf_op jit(solution)/shard_map/while/body/eval_jaxpr/all_gather | solution.py:114
  3049.5 87.0 %all-gather.19.cloned.1.call-start = ((), (), s32[]{:S(2)}) async-start(), calls=%async_computation.24 | async-start | bytes 1638400 | tf_op jit(solution)/shard_map/while/body/eval_jaxpr/all_gather | solution.py:114
  3145.2 87.0 %all-gather.19.cloned.1.call-start = ((), (), s32[]{:S(2)}) async-start(), calls=%async_computation.24 | async-start | bytes 1638400 | tf_op jit(solution)/shard_map/while/body/eval_jaxpr/all_gather | solution.py:114
  3240.9 87.0 %all-gather.19.cloned.1.call-start = ((), (), s32[]{:S(2)}) async-start(), calls=%async_computation.24 | async-start | bytes 1638400 | tf_op jit(solution)/shard_map/while/body/eval_jaxpr/all_gather | solution.py:114
  3336.6 87.0 %all-gather.19.cloned.1.call-start = ((), (), s32[]{:S(2)}) async-start(), calls=%async_computation.24 | async-start | bytes 1638400 | tf_op jit(solution)/shard_map/while/body/eval_jaxpr/all_gather | solution.py:114
  3432.3 87.0 %all-gather.19.cloned.1.call-start = ((), (), s32[]{:S(2)}) async-start(), calls=%async_computation.24 | async-start | bytes 1638400 | tf_op jit(solution)/shard_map/while/body/eval_jaxpr/all_gather | solution.py:114
  3528.0 87.0 %all-gather.19.cloned.1.call-start = ((), (), s32[]{:S(2)}) async-start(), calls=%async_computation.24 | async-start | bytes 1638400 | tf_op jit(solution)/shard_map/while/body/eval_jaxpr/all_gather | solution.py:114
  3623.7 87.0 %all-gather.19.cloned.1.call-start = ((), (), s32[]{:S(2)}) async-start(), calls=%async_computation.24 | async-start | bytes 1638400 | tf_op jit(solution)/shard_map/while/body/eval_jaxpr/all_gather | solution.py:114
  3719.4 87.0 %all-gather.19.cloned.1.call-start = ((), (), s32[]{:S(2)}) async-start(), calls=%async_computation.24 | async-start | bytes 1638400 | tf_op jit(solution)/shard_map/while/body/eval_jaxpr/all_gather | solution.py:114
  3809.0 77.9 %all-gather.17.cloned.1.call-start = ((), (), s32[]{:S(2)}) async-start(), calls=%async_computation.15 | async-start | bytes 4915200 | tf_op jit(solution)/shard_map/all_gather | solution.py:192
  3809.7 120.9 %all-gather.15.cloned.1.call-start = ((), (), s32[]{:S(2)}) async-start(), calls=%async_computation.14 | async-start | bytes 2457600 | tf_op jit(solution)/shard_map/all_gather | solution.py:161
  3811.6 537.6 %all-reduce.2.cloned.1.call-start = ((), (), s32[]{:S(2)}) async-start(), calls=%async_computation.16 | async-start | bytes 3932160 | tf_op jit(solution)/shard_map/psum | solution.py:211
  4268.3 117.7 %reduce-scatter.31.cloned.1.call-start = ((), (), s32[]{:S(2)}) async-start(), calls=%async_computation.22 | async-start | bytes 737280
  4271.6 155.6 %reduce-scatter.29.cloned.1.call-start = ((), (), s32[]{:S(2)}) async-start(), calls=%async_computation.21 | async-start | bytes 1474560
  4281.7 182.2 %reduce-scatter.27.cloned.1.call-start = ((), (), s32[]{:S(2)}) async-start(), calls=%async_computation.20 | async-start | bytes 368640
  4356.3 144.4 %reduce-scatter.25.cloned.1.call-start = ((), (), s32[]{:S(2)}) async-start(), calls=%async_computation.19 | async-start | bytes 368640
  4357.3 194.1 %reduce-scatter.21.cloned.1.call-start = ((), (), s32[]{:S(2)}) async-start(), calls=%async_computation.17 | async-start | bytes 3686400 | tf_op jit(solution)/shard_map/reduce_scatter | solution.py:194
  4357.9 244.4 %reduce-scatter.23.cloned.1.call-start = ((), (), s32[]{:S(2)}) async-start(), calls=%async_computation.18 | async-start | bytes 3686400 | tf_op jit(solution)/shard_map/reduce_scatter | solution.py:195
  (123 other events, 4937.4 us)
Sparse Core Ops, SparseCore 0:
  232.7 72.9 reduce-scatter.18
  308.5 76.8 all-gather.8
  445.9 52.0 reduce-scatter.36
  500.2 51.7 reduce-scatter.34
  630.8 51.0 reduce-scatter.36
  684.1 51.7 reduce-scatter.34
  815.5 51.0 reduce-scatter.36
  868.8 51.7 reduce-scatter.34
  923.1 32.3 all-gather.20
  1000.3 51.0 reduce-scatter.36
  1053.6 51.7 reduce-scatter.34
  1107.8 32.3 all-gather.20
  1185.0 51.0 reduce-scatter.36
  1238.4 51.7 reduce-scatter.34
  1292.7 32.3 all-gather.20
  1369.9 51.0 reduce-scatter.36
  1423.2 51.7 reduce-scatter.34
  1554.7 51.0 reduce-scatter.36
  1608.0 51.7 reduce-scatter.34
  1662.3 32.3 all-gather.20
  1739.6 51.0 reduce-scatter.36
  1793.1 51.7 reduce-scatter.34
  1924.5 51.0 reduce-scatter.36
  1977.9 51.7 reduce-scatter.34
  2032.2 32.3 all-gather.20
  2109.5 51.0 reduce-scatter.36
  2162.9 51.7 reduce-scatter.34
  2217.2 32.3 all-gather.20
  2294.5 51.1 reduce-scatter.36
  2347.8 51.7 reduce-scatter.34
  2479.2 51.0 reduce-scatter.36
  2532.7 51.7 reduce-scatter.34
  2586.9 32.3 all-gather.20
  2666.8 51.1 reduce-scatter.32
  2762.5 51.0 reduce-scatter.32
  2817.0 32.3 all-gather.18
  2858.2 51.0 reduce-scatter.32
  2912.7 32.3 all-gather.18
  2953.9 51.0 reduce-scatter.32
  3008.4 32.3 all-gather.18
  3049.6 51.0 reduce-scatter.32
  3104.1 32.3 all-gather.18
  3145.3 51.0 reduce-scatter.32
  3199.8 32.3 all-gather.18
  3241.0 51.0 reduce-scatter.32
  3295.5 32.3 all-gather.18
  3336.7 51.0 reduce-scatter.32
  3391.2 32.3 all-gather.18
  3432.4 51.0 reduce-scatter.32
  3486.9 32.3 all-gather.18
  3528.1 51.0 reduce-scatter.32
  3582.6 32.3 all-gather.18
  3623.9 51.0 reduce-scatter.32
  3719.6 51.0 reduce-scatter.32
  3774.0 32.3 all-gather.18
  3811.4 75.4 all-gather.16
  3888.4 42.1 all-gather.14
  4268.5 80.7 all-reduce.1
  4352.4 33.5 reduce-scatter.30
  4389.8 37.3 reduce-scatter.28
  4430.1 33.7 reduce-scatter.26
  4466.9 33.7 reduce-scatter.24
  4504.6 46.8 reduce-scatter.20
  4555.4 46.8 reduce-scatter.22
  (21 shorter events, 656.2 us)
where the time goes:
time: 4630 us; the launch traced here: 4610 us
  waiting for transfers between devices  3470 us (75%)
  matrix products  501 us (11%)
  local copies, waits for them, and re-layouts  284 us (6%)
  other arithmetic  192 us (4%)
  loops' own time  119 us (3%)
    reduce_scatter x24, waiting for transfers between devices, hidden_block(): lax.psum_scatter(jnp.dot(x_block, ffn_in_full, preferred_element_type=jnp...  1200 us
    all_gather x24, waiting for transfers between devices, hidden_block(): act_rows = lax.all_gather(act_share, 'narrow', axis=0, tiled=True)  675 us
    reduce_scatter x12, waiting for transfers between devices, ffn_backward(): lax.psum_scatter(jnp.dot(dy_block, ffn_down_part, preferred_element_type=...  610 us
    all_gather x12, waiting for transfers between devices, ffn_backward(): drows = lax.all_gather(dshare, 'narrow', axis=0, tiled=True)  382 us
    unnamed x17, waiting for transfers between devices  126 us
  transfers between devices with their start and end apart: 85, of which 85 were waited for; matrix products, arithmetic and copies ran while one was open for 5% of the time, Pallas kernels for 0%

commit v1 on v0

--- a/solution.py
+++ b/solution.py
@@ -175,7 +175,13 @@
         )
         _, gelu_back = jax.vjp(partial(jax.nn.gelu, approximate=False), share)
         dshare = gelu_back(dact)[0].astype(jnp.bfloat16)
-        drows = lax.all_gather(dshare, "narrow", axis=0, tiled=True)
+        devices = lax.axis_size("narrow")
+        held, tiles = (dshare, [dshare])
+        for _ in range(devices - 1):
+            held = lax.ppermute(held, "narrow", [(i, (i + 1) % devices) for i in range(devices)])
+            tiles.insert(0, held)
+        line = jnp.concatenate(tiles, axis=0)
+        drows = jnp.roll(line, (lax.axis_index("narrow") + 1) * dshare.shape[0], axis=0)
         grad_in = grad_in + lax.dot_general(
             x_block, drows, (((0,), (0,)), ((), ())), preferred_element_type=jnp.float32
         )

time: 4630 us -> 4480 us (0.968)
  waiting for transfers between devices: 3470 us -> 3320 us
    all_gather x12 -> x0, waiting for transfers between devices: 382 us -> none  [ffn_backward(): drows = lax.all_gather(dshare, 'narrow', axis=0, tiled=True)]
    ppermute x0 -> x36, waiting for transfers between devices: none -> 358 us  [ffn_backward(): lax.ppermute(held, 'narrow', [(i, (i + 1) % devices) for i in range(devic...]
    all_gather x24, waiting for transfers between devices: 675 us -> 567 us  [hidden_block(): act_rows = lax.all_gather(act_share, 'narrow', axis=0, tiled=True)]
  transfers between devices with their start and end apart: 85 -> 109, of which waited for: 85 -> 109; matrix products, arithmetic and copies ran while one was open for 5% -> 6% of each run, Pallas kernels for 0% -> 0%
where the time goes in v1:
time: 4480 us; the launch traced here: 4470 us
  waiting for transfers between devices  3320 us (74%)
  matrix products  476 us (11%)
  local copies, waits for them, and re-layouts  318 us (7%)
  other arithmetic  183 us (4%)
  loops' own time  119 us (3%)
    reduce_scatter x24, waiting for transfers between devices, hidden_block(): lax.psum_scatter(jnp.dot(x_block, ffn_in_full, preferred_element_type=jnp...  1190 us
    reduce_scatter x12, waiting for transfers between devices, ffn_backward(): lax.psum_scatter(jnp.dot(dy_block, ffn_down_part, preferred_element_type=...  610 us
    all_gather x24, waiting for transfers between devices, hidden_block(): act_rows = lax.all_gather(act_share, 'narrow', axis=0, tiled=True)  567 us
    ppermute x36, waiting for transfers between devices, ffn_backward(): lax.ppermute(held, 'narrow', [(i, (i + 1) % devices) for i in range(devic...  358 us
    unnamed x17, waiting for transfers between devices  126 us
  transfers between devices with their start and end apart: 109, of which 109 were waited for; matrix products, arithmetic and copies ran while one was open for 6% of the time, Pallas kernels for 0%

profile of v1, /device:TPU:0, one launch (start us, length us, event | category | flops | bytes accessed | tf_op | source)
XLA Modules:
  0.0 4465.4 jit_solution(13923830024157500371)
XLA Ops:
  36.0 183.3 %while.86 = (s32[]{:T(128)}, bf16[5,1536,32]{1,2,0:T(8,128)(2,1)}, f32[5,1536]{1,0:T(8,128)}, s32[5]{0:T(128)}, bf16[1536,160]{1,0:T(8,128)(2,1)}, /*index=5*/bf...) while((s32[]{:T(128)}, bf16[5,1536,32]{1,2,0:T(8,128)(2,1)}, ...), condition=%wide.region_9.10_spmd.clone, body=%wide.region_4.9_spmd.clone.sunk | while | flops 107740680 | bytes 11363814 | solution.py:55
  237.3 69.2 %reduce-scatter.19.cloned.1.call-done = f32[1536,160]{0,1:T(8,128)} async-done(((f32[1536,640]{0,1:T(8,128)}), f32[1536,160]{0,1:T(8,128)}) %reduce-scatter.19.cloned.1.call-update) | async-done | bytes 983056 | tf_op jit(solution)/shard_map/reduce_scatter | solution.py:141
  313.8 72.3 %all-gather.8.cloned.1.call-done = f32[1536,640]{0,1:T(8,128)} async-done(((f32[1536,160]{0,1:T(8,128)}), f32[1536,640]{0,1:T(8,128)}) %all-gather.8.cloned.1.call-update) | async-done | bytes 3932176 | tf_op jit(solution)/shard_map/all_gather | solution.py:143
  440.3 2076.3 %while.89 = (s32[]{:T(128)}, f32[160,5120]{1,0:T(8,128)}, f32[160,5120]{1,0:T(8,128)}, f32[12,128,160]{1,0,2:T(8,128)}, s32[12]{0:T(128)S(1)}, /*index=5*/bf16[1...) while((s32[]{:T(128)}, f32[160,5120]{1,0:T(8,128)}, ...), condition=%wide.region_19.20_spmd.clone, body=%wide.region_16.19_spmd.clone.sunk | while | flops 1064796160 | bytes 115196736 | solution.py:197
  449.5 49.3 %reduce-scatter.37.cloned.1.call-done = f32[32,5120]{1,0:T(8,128)} async-done(((f32[128,5120]{1,0:T(8,128)}), f32[32,5120]{1,0:T(8,128)}) %reduce-scatter.37.cloned.1.call-update) | async-done | bytes 655376 | tf_op jit(solution)/shard_map/while/body/eval_jaxpr/reduce_scatter | solution.py:107
  501.9 50.8 %reduce-scatter.35.cloned.1.call-done = f32[32,5120]{1,0:T(8,128)} async-done(((f32[128,5120]{1,0:T(8,128)}), f32[32,5120]{1,0:T(8,128)}) %reduce-scatter.35.cloned.1.call-update) | async-done | bytes 655376 | tf_op jit(solution)/shard_map/while/body/eval_jaxpr/reduce_scatter | solution.py:170
  623.4 48.3 %reduce-scatter.37.cloned.1.call-done = f32[32,5120]{1,0:T(8,128)} async-done(((f32[128,5120]{1,0:T(8,128)}), f32[32,5120]{1,0:T(8,128)}) %reduce-scatter.37.cloned.1.call-update) | async-done | bytes 655376 | tf_op jit(solution)/shard_map/while/body/eval_jaxpr/reduce_scatter | solution.py:107
  674.8 50.9 %reduce-scatter.35.cloned.1.call-done = f32[32,5120]{1,0:T(8,128)} async-done(((f32[128,5120]{1,0:T(8,128)}), f32[32,5120]{1,0:T(8,128)}) %reduce-scatter.35.cloned.1.call-update) | async-done | bytes 655376 | tf_op jit(solution)/shard_map/while/body/eval_jaxpr/reduce_scatter | solution.py:170
  796.5 48.3 %reduce-scatter.37.cloned.1.call-done = f32[32,5120]{1,0:T(8,128)} async-done(((f32[128,5120]{1,0:T(8,128)}), f32[32,5120]{1,0:T(8,128)}) %reduce-scatter.37.cloned.1.call-update) | async-done | bytes 655376 | tf_op jit(solution)/shard_map/while/body/eval_jaxpr/reduce_scatter | solution.py:107
  848.0 50.8 %reduce-scatter.35.cloned.1.call-done = f32[32,5120]{1,0:T(8,128)} async-done(((f32[128,5120]{1,0:T(8,128)}), f32[32,5120]{1,0:T(8,128)}) %reduce-scatter.35.cloned.1.call-update) | async-done | bytes 655376 | tf_op jit(solution)/shard_map/while/body/eval_jaxpr/reduce_scatter | solution.py:170
  969.4 48.3 %reduce-scatter.37.cloned.1.call-done = f32[32,5120]{1,0:T(8,128)} async-done(((f32[128,5120]{1,0:T(8,128)}), f32[32,5120]{1,0:T(8,128)}) %reduce-scatter.37.cloned.1.call-update) | async-done | bytes 655376 | tf_op jit(solution)/shard_map/while/body/eval_jaxpr/reduce_scatter | solution.py:107
  1020.8 50.8 %reduce-scatter.35.cloned.1.call-done = f32[32,5120]{1,0:T(8,128)} async-done(((f32[128,5120]{1,0:T(8,128)}), f32[32,5120]{1,0:T(8,128)}) %reduce-scatter.35.cloned.1.call-update) | async-done | bytes 655376 | tf_op jit(solution)/shard_map/while/body/eval_jaxpr/reduce_scatter | solution.py:170
  1142.4 48.2 %reduce-scatter.37.cloned.1.call-done = f32[32,5120]{1,0:T(8,128)} async-done(((f32[128,5120]{1,0:T(8,128)}), f32[32,5120]{1,0:T(8,128)}) %reduce-scatter.37.cloned.1.call-update) | async-done | bytes 655376 | tf_op jit(solution)/shard_map/while/body/eval_jaxpr/reduce_scatter | solution.py:107
  1193.8 50.8 %reduce-scatter.35.cloned.1.call-done = f32[32,5120]{1,0:T(8,128)} async-done(((f32[128,5120]{1,0:T(8,128)}), f32[32,5120]{1,0:T(8,128)}) %reduce-scatter.35.cloned.1.call-update) | async-done | bytes 655376 | tf_op jit(solution)/shard_map/while/body/eval_jaxpr/reduce_scatter | solution.py:170
  1315.3 48.2 %reduce-scatter.37.cloned.1.call-done = f32[32,5120]{1,0:T(8,128)} async-done(((f32[128,5120]{1,0:T(8,128)}), f32[32,5120]{1,0:T(8,128)}) %reduce-scatter.37.cloned.1.call-update) | async-done | bytes 655376 | tf_op jit(solution)/shard_map/while/body/eval_jaxpr/reduce_scatter | solution.py:107
  1366.7 50.9 %reduce-scatter.35.cloned.1.call-done = f32[32,5120]{1,0:T(8,128)} async-done(((f32[128,5120]{1,0:T(8,128)}), f32[32,5120]{1,0:T(8,128)}) %reduce-scatter.35.cloned.1.call-update) | async-done | bytes 655376 | tf_op jit(solution)/shard_map/while/body/eval_jaxpr/reduce_scatter | solution.py:170
  1488.3 48.3 %reduce-scatter.37.cloned.1.call-done = f32[32,5120]{1,0:T(8,128)} async-done(((f32[128,5120]{1,0:T(8,128)}), f32[32,5120]{1,0:T(8,128)}) %reduce-scatter.37.cloned.1.call-update) | async-done | bytes 655376 | tf_op jit(solution)/shard_map/while/body/eval_jaxpr/reduce_scatter | solution.py:107
  1539.8 50.8 %reduce-scatter.35.cloned.1.call-done = f32[32,5120]{1,0:T(8,128)} async-done(((f32[128,5120]{1,0:T(8,128)}), f32[32,5120]{1,0:T(8,128)}) %reduce-scatter.35.cloned.1.call-update) | async-done | bytes 655376 | tf_op jit(solution)/shard_map/while/body/eval_jaxpr/reduce_scatter | solution.py:170
  1661.2 48.3 %reduce-scatter.37.cloned.1.call-done = f32[32,5120]{1,0:T(8,128)} async-done(((f32[128,5120]{1,0:T(8,128)}), f32[32,5120]{1,0:T(8,128)}) %reduce-scatter.37.cloned.1.call-update) | async-done | bytes 655376 | tf_op jit(solution)/shard_map/while/body/eval_jaxpr/reduce_scatter | solution.py:107
  1712.7 50.8 %reduce-scatter.35.cloned.1.call-done = f32[32,5120]{1,0:T(8,128)} async-done(((f32[128,5120]{1,0:T(8,128)}), f32[32,5120]{1,0:T(8,128)}) %reduce-scatter.35.cloned.1.call-update) | async-done | bytes 655376 | tf_op jit(solution)/shard_map/while/body/eval_jaxpr/reduce_scatter | solution.py:170
  1834.1 48.3 %reduce-scatter.37.cloned.1.call-done = f32[32,5120]{1,0:T(8,128)} async-done(((f32[128,5120]{1,0:T(8,128)}), f32[32,5120]{1,0:T(8,128)}) %reduce-scatter.37.cloned.1.call-update) | async-done | bytes 655376 | tf_op jit(solution)/shard_map/while/body/eval_jaxpr/reduce_scatter | solution.py:107
  1885.6 50.8 %reduce-scatter.35.cloned.1.call-done = f32[32,5120]{1,0:T(8,128)} async-done(((f32[128,5120]{1,0:T(8,128)}), f32[32,5120]{1,0:T(8,128)}) %reduce-scatter.35.cloned.1.call-update) | async-done | bytes 655376 | tf_op jit(solution)/shard_map/while/body/eval_jaxpr/reduce_scatter | solution.py:170
  2007.1 48.3 %reduce-scatter.37.cloned.1.call-done = f32[32,5120]{1,0:T(8,128)} async-done(((f32[128,5120]{1,0:T(8,128)}), f32[32,5120]{1,0:T(8,128)}) %reduce-scatter.37.cloned.1.call-update) | async-done | bytes 655376 | tf_op jit(solution)/shard_map/while/body/eval_jaxpr/reduce_scatter | solution.py:107
  2058.5 50.8 %reduce-scatter.35.cloned.1.call-done = f32[32,5120]{1,0:T(8,128)} async-done(((f32[128,5120]{1,0:T(8,128)}), f32[32,5120]{1,0:T(8,128)}) %reduce-scatter.35.cloned.1.call-update) | async-done | bytes 655376 | tf_op jit(solution)/shard_map/while/body/eval_jaxpr/reduce_scatter | solution.py:170
  2180.0 48.3 %reduce-scatter.37.cloned.1.call-done = f32[32,5120]{1,0:T(8,128)} async-done(((f32[128,5120]{1,0:T(8,128)}), f32[32,5120]{1,0:T(8,128)}) %reduce-scatter.37.cloned.1.call-update) | async-done | bytes 655376 | tf_op jit(solution)/shard_map/while/body/eval_jaxpr/reduce_scatter | solution.py:107
  2231.4 50.8 %reduce-scatter.35.cloned.1.call-done = f32[32,5120]{1,0:T(8,128)} async-done(((f32[128,5120]{1,0:T(8,128)}), f32[32,5120]{1,0:T(8,128)}) %reduce-scatter.35.cloned.1.call-update) | async-done | bytes 655376 | tf_op jit(solution)/shard_map/while/body/eval_jaxpr/reduce_scatter | solution.py:170
  2352.8 48.3 %reduce-scatter.37.cloned.1.call-done = f32[32,5120]{1,0:T(8,128)} async-done(((f32[128,5120]{1,0:T(8,128)}), f32[32,5120]{1,0:T(8,128)}) %reduce-scatter.37.cloned.1.call-update) | async-done | bytes 655376 | tf_op jit(solution)/shard_map/while/body/eval_jaxpr/reduce_scatter | solution.py:107
  2404.3 50.8 %reduce-scatter.35.cloned.1.call-done = f32[32,5120]{1,0:T(8,128)} async-done(((f32[128,5120]{1,0:T(8,128)}), f32[32,5120]{1,0:T(8,128)}) %reduce-scatter.35.cloned.1.call-update) | async-done | bytes 655376 | tf_op jit(solution)/shard_map/while/body/eval_jaxpr/reduce_scatter | solution.py:170
  2519.2 1148.3 %while.84 = (s32[]{:T(128)}, bf16[12,128,160]{1,2,0:T(8,128)(2,1)}, s32[12]{0:T(128)S(1)}, bf16[1536,160]{1,0:T(8,128)(2,1)}, bf16[160,5120]{1,0:T(8,128)(2,1)},...) while((s32[]{:T(128)}, bf16[12,128,160]{1,2,0:T(8,128)(2,1)}, s32[12]{0:T(128)S(1)}, ...), condition=%wide.region_15.16_spmd, body=%wide.region_13.15_spmd.sunk | while | flops 430080000 | bytes 29638920 | solution.py:160
  2525.4 51.2 %reduce-scatter.33.cloned.1.call-done = f32[32,5120]{1,0:T(8,128)} async-done(((f32[128,5120]{1,0:T(8,128)}), f32[32,5120]{1,0:T(8,128)}) %reduce-scatter.33.cloned.1.call-update) | async-done | bytes 655376 | tf_op jit(solution)/shard_map/while/body/eval_jaxpr/reduce_scatter | solution.py:107
  2579.9 32.5 all-gather.18.cloned.1.call-done
  2621.1 51.2 %reduce-scatter.33.cloned.1.call-done = f32[32,5120]{1,0:T(8,128)} async-done(((f32[128,5120]{1,0:T(8,128)}), f32[32,5120]{1,0:T(8,128)}) %reduce-scatter.33.cloned.1.call-update) | async-done | bytes 655376 | tf_op jit(solution)/shard_map/while/body/eval_jaxpr/reduce_scatter | solution.py:107
  2675.6 32.5 all-gather.18.cloned.1.call-done
  2716.8 51.2 %reduce-scatter.33.cloned.1.call-done = f32[32,5120]{1,0:T(8,128)} async-done(((f32[128,5120]{1,0:T(8,128)}), f32[32,5120]{1,0:T(8,128)}) %reduce-scatter.33.cloned.1.call-update) | async-done | bytes 655376 | tf_op jit(solution)/shard_map/while/body/eval_jaxpr/reduce_scatter | solution.py:107
  2771.3 32.6 all-gather.18.cloned.1.call-done
  2812.5 51.2 %reduce-scatter.33.cloned.1.call-done = f32[32,5120]{1,0:T(8,128)} async-done(((f32[128,5120]{1,0:T(8,128)}), f32[32,5120]{1,0:T(8,128)}) %reduce-scatter.33.cloned.1.call-update) | async-done | bytes 655376 | tf_op jit(solution)/shard_map/while/body/eval_jaxpr/reduce_scatter | solution.py:107
  2908.2 51.2 %reduce-scatter.33.cloned.1.call-done = f32[32,5120]{1,0:T(8,128)} async-done(((f32[128,5120]{1,0:T(8,128)}), f32[32,5120]{1,0:T(8,128)}) %reduce-scatter.33.cloned.1.call-update) | async-done | bytes 655376 | tf_op jit(solution)/shard_map/while/body/eval_jaxpr/reduce_scatter | solution.py:107
  3003.9 51.2 %reduce-scatter.33.cloned.1.call-done = f32[32,5120]{1,0:T(8,128)} async-done(((f32[128,5120]{1,0:T(8,128)}), f32[32,5120]{1,0:T(8,128)}) %reduce-scatter.33.cloned.1.call-update) | async-done | bytes 655376 | tf_op jit(solution)/shard_map/while/body/eval_jaxpr/reduce_scatter | solution.py:107
  3058.3 32.5 all-gather.18.cloned.1.call-done
  3099.6 51.2 %reduce-scatter.33.cloned.1.call-done = f32[32,5120]{1,0:T(8,128)} async-done(((f32[128,5120]{1,0:T(8,128)}), f32[32,5120]{1,0:T(8,128)}) %reduce-scatter.33.cloned.1.call-update) | async-done | bytes 655376 | tf_op jit(solution)/shard_map/while/body/eval_jaxpr/reduce_scatter | solution.py:107
  3154.0 32.5 all-gather.18.cloned.1.call-done
  3195.3 51.2 %reduce-scatter.33.cloned.1.call-done = f32[32,5120]{1,0:T(8,128)} async-done(((f32[128,5120]{1,0:T(8,128)}), f32[32,5120]{1,0:T(8,128)}) %reduce-scatter.33.cloned.1.call-update) | async-done | bytes 655376 | tf_op jit(solution)/shard_map/while/body/eval_jaxpr/reduce_scatter | solution.py:107
  3249.7 32.5 all-gather.18.cloned.1.call-done
  3291.0 51.2 %reduce-scatter.33.cloned.1.call-done = f32[32,5120]{1,0:T(8,128)} async-done(((f32[128,5120]{1,0:T(8,128)}), f32[32,5120]{1,0:T(8,128)}) %reduce-scatter.33.cloned.1.call-update) | async-done | bytes 655376 | tf_op jit(solution)/shard_map/while/body/eval_jaxpr/reduce_scatter | solution.py:107
  3345.4 32.5 all-gather.18.cloned.1.call-done
  3386.6 51.2 %reduce-scatter.33.cloned.1.call-done = f32[32,5120]{1,0:T(8,128)} async-done(((f32[128,5120]{1,0:T(8,128)}), f32[32,5120]{1,0:T(8,128)}) %reduce-scatter.33.cloned.1.call-update) | async-done | bytes 655376 | tf_op jit(solution)/shard_map/while/body/eval_jaxpr/reduce_scatter | solution.py:107
  3441.1 32.5 all-gather.18.cloned.1.call-done
  3482.3 51.2 %reduce-scatter.33.cloned.1.call-done = f32[32,5120]{1,0:T(8,128)} async-done(((f32[128,5120]{1,0:T(8,128)}), f32[32,5120]{1,0:T(8,128)}) %reduce-scatter.33.cloned.1.call-update) | async-done | bytes 655376 | tf_op jit(solution)/shard_map/while/body/eval_jaxpr/reduce_scatter | solution.py:107
  3536.7 32.6 all-gather.18.cloned.1.call-done
  3578.0 51.2 %reduce-scatter.33.cloned.1.call-done = f32[32,5120]{1,0:T(8,128)} async-done(((f32[128,5120]{1,0:T(8,128)}), f32[32,5120]{1,0:T(8,128)}) %reduce-scatter.33.cloned.1.call-update) | async-done | bytes 655376 | tf_op jit(solution)/shard_map/while/body/eval_jaxpr/reduce_scatter | solution.py:107
  3632.4 32.6 all-gather.18.cloned.1.call-done
  3673.1 72.3 %all-gather.16.cloned.1.call-done = f32[1536,640]{0,1:T(8,128)} async-done(((f32[1536,160]{0,1:T(8,128)}), f32[1536,640]{0,1:T(8,128)}) %all-gather.16.cloned.1.call-update) | async-done | bytes 3932176 | tf_op jit(solution)/shard_map/all_gather | solution.py:198
  3750.6 38.3 all-gather.14.cloned.1.call-done
  3801.0 317.2 %while.88 = (s32[]{:T(128)}, bf16[5,1536,32]{2,1,0:T(8,128)(2,1)}, bf16[5,1536,32]{1,2,0:T(8,128)(2,1)}, bf16[5,1536,32]{1,2,0:T(8,128)(2,1)}, s32[5]{0:T(128)},...) while((s32[]{:T(128)}, bf16[5,1536,32]{2,1,0:T(8,128)(2,1)}, ...), condition=%wide.region_26.27_spmd.clone, body=%wide.region_22.26_spmd.clone.sunk | while | flops 259784208 | bytes 27660404 | solution.py:97
  3812.9 48.0 %while.91 = (s32[]{:T(128)}, f32[1536,32]{0,1:T(8,128)}, f32[1536,32]{0,1:T(8,128)}, bf16[3,512,32]{1,2,0:T(8,128)(2,1)}, s32[3]{0:T(128)}, /*index=5*/s32[1536]...) while((s32[]{:T(128)}, f32[1536,32]{0,1:T(8,128)}, ...), condition=%wide.region_25.25_spmd.clone, body=%wide.region_23.24_spmd.clone.sunk | while | flops 259784192 | bytes 25385684 | solution.py:94
  3876.3 48.0 %while.91 = (s32[]{:T(128)}, f32[1536,32]{0,1:T(8,128)}, f32[1536,32]{0,1:T(8,128)}, bf16[3,512,32]{1,2,0:T(8,128)(2,1)}, s32[3]{0:T(128)}, /*index=5*/s32[1536]...) while((s32[]{:T(128)}, f32[1536,32]{0,1:T(8,128)}, ...), condition=%wide.region_25.25_spmd.clone, body=%wide.region_23.24_spmd.clone.sunk | while | flops 259784192 | bytes 25385684 | solution.py:94
  3939.7 48.0 %while.91 = (s32[]{:T(128)}, f32[1536,32]{0,1:T(8,128)}, f32[1536,32]{0,1:T(8,128)}, bf16[3,512,32]{1,2,0:T(8,128)(2,1)}, s32[3]{0:T(128)}, /*index=5*/s32[1536]...) while((s32[]{:T(128)}, f32[1536,32]{0,1:T(8,128)}, ...), condition=%wide.region_25.25_spmd.clone, body=%wide.region_23.24_spmd.clone.sunk | while | flops 259784192 | bytes 25385684 | solution.py:94
  4003.2 48.0 %while.91 = (s32[]{:T(128)}, f32[1536,32]{0,1:T(8,128)}, f32[1536,32]{0,1:T(8,128)}, bf16[3,512,32]{1,2,0:T(8,128)(2,1)}, s32[3]{0:T(128)}, /*index=5*/s32[1536]...) while((s32[]{:T(128)}, f32[1536,32]{0,1:T(8,128)}, ...), condition=%wide.region_25.25_spmd.clone, body=%wide.region_23.24_spmd.clone.sunk | while | flops 259784192 | bytes 25385684 | solution.py:94
  4066.6 48.0 %while.91 = (s32[]{:T(128)}, f32[1536,32]{0,1:T(8,128)}, f32[1536,32]{0,1:T(8,128)}, bf16[3,512,32]{1,2,0:T(8,128)(2,1)}, s32[3]{0:T(128)}, /*index=5*/s32[1536]...) while((s32[]{:T(128)}, f32[1536,32]{0,1:T(8,128)}, ...), condition=%wide.region_25.25_spmd.clone, body=%wide.region_23.24_spmd.clone.sunk | while | flops 259784192 | bytes 25385684 | solution.py:94
  4138.3 67.4 %all-reduce.2.cloned.1.call-done = bf16[1536,640]{0,1:T(8,128)(2,1)} async-done(((bf16[1536,640]{0,1:T(8,128)(2,1)}), bf16[1536,640]{0,1:T(8,128)(2,1)}) %all-reduce.2.cloned.1.call-update) | async-done | bytes 1966096 | tf_op jit(solution)/shard_map/psum | solution.py:217
  4244.1 39.6 reduce-scatter.29.cloned.1.call-done
  4321.8 35.4 reduce-scatter.25.cloned.1.call-done
  4358.6 49.3 %reduce-scatter.21.cloned.1.call-done = f32[160,640]{1,0:T(8,128)} async-done(((f32[160,5120]{1,0:T(8,128)}), f32[160,640]{1,0:T(8,128)}) %reduce-scatter.21.cloned.1.call-update) | async-done | bytes 409616 | tf_op jit(solution)/shard_map/reduce_scatter | solution.py:200
  4407.9 50.7 %reduce-scatter.23.cloned.1.call-done = f32[160,640]{1,0:T(8,128)} async-done(((f32[160,5120]{1,0:T(8,128)}), f32[160,640]{1,0:T(8,128)}) %reduce-scatter.23.cloned.1.call-update) | async-done | bytes 409616 | tf_op jit(solution)/shard_map/reduce_scatter | solution.py:201
  (1140 shorter events, 1837.7 us)
Async XLA Ops:
  7.2 299.3 %reduce-scatter.19.cloned.1.call-start = ((), (), s32[]{:S(2)}) async-start(), calls=%async_computation.10 | async-start | bytes 4915200 | tf_op jit(solution)/shard_map/reduce_scatter | solution.py:141
  233.4 152.7 %all-gather.8.cloned.1.call-start = ((), (), s32[]{:S(2)}) async-start(), calls=%async_computation.11 | async-start | bytes 4915200 | tf_op jit(solution)/shard_map/all_gather | solution.py:143
  309.1 103.5 %all-gather.10.cloned.1.call-start = ((), (), s32[]{:S(2)}) async-start(), calls=%async_computation.12 | async-start | bytes 1843200 | tf_op jit(solution)/shard_map/all_gather | solution.py:146
  309.8 130.5 %all-gather.12.cloned.1.call-start = ((), (), s32[]{:S(2)}) async-start(), calls=%async_computation.13 | async-start | bytes 1843200 | tf_op jit(solution)/shard_map/all_gather | solution.py:147
  440.3 58.4 %reduce-scatter.37.cloned.1.call-start = ((), (), s32[]{:S(2)}) async-start(), calls=%async_computation.26 | async-start | bytes 3276800 | tf_op jit(solution)/shard_map/while/body/eval_jaxpr/reduce_scatter | solution.py:107
  446.5 106.3 %reduce-scatter.35.cloned.1.call-start = ((), (), s32[]{:S(2)}) async-start(), calls=%async_computation.25 | async-start | bytes 3276800 | tf_op jit(solution)/shard_map/while/body/eval_jaxpr/reduce_scatter | solution.py:170
  449.4 160.5 %all-gather.20.cloned.1.call-start = ((), (), s32[]{:S(2)}) async-start(), calls=%async_computation.27 | async-start | bytes 1638400 | tf_op jit(solution)/shard_map/while/body/eval_jaxpr/all_gather | solution.py:114
  614.2 57.4 %reduce-scatter.37.cloned.1.call-start = ((), (), s32[]{:S(2)}) async-start(), calls=%async_computation.26 | async-start | bytes 3276800 | tf_op jit(solution)/shard_map/while/body/eval_jaxpr/reduce_scatter | solution.py:107
  620.4 105.4 %reduce-scatter.35.cloned.1.call-start = ((), (), s32[]{:S(2)}) async-start(), calls=%async_computation.25 | async-start | bytes 3276800 | tf_op jit(solution)/shard_map/while/body/eval_jaxpr/reduce_scatter | solution.py:170
  623.3 159.6 %all-gather.20.cloned.1.call-start = ((), (), s32[]{:S(2)}) async-start(), calls=%async_computation.27 | async-start | bytes 1638400 | tf_op jit(solution)/shard_map/while/body/eval_jaxpr/all_gather | solution.py:114
  787.3 57.4 %reduce-scatter.37.cloned.1.call-start = ((), (), s32[]{:S(2)}) async-start(), calls=%async_computation.26 | async-start | bytes 3276800 | tf_op jit(solution)/shard_map/while/body/eval_jaxpr/reduce_scatter | solution.py:107
  793.5 105.2 %reduce-scatter.35.cloned.1.call-start = ((), (), s32[]{:S(2)}) async-start(), calls=%async_computation.25 | async-start | bytes 3276800 | tf_op jit(solution)/shard_map/while/body/eval_jaxpr/reduce_scatter | solution.py:170
  796.4 159.5 %all-gather.20.cloned.1.call-start = ((), (), s32[]{:S(2)}) async-start(), calls=%async_computation.27 | async-start | bytes 1638400 | tf_op jit(solution)/shard_map/while/body/eval_jaxpr/all_gather | solution.py:114
  960.2 57.4 %reduce-scatter.37.cloned.1.call-start = ((), (), s32[]{:S(2)}) async-start(), calls=%async_computation.26 | async-start | bytes 3276800 | tf_op jit(solution)/shard_map/while/body/eval_jaxpr/reduce_scatter | solution.py:107
  966.4 105.2 %reduce-scatter.35.cloned.1.call-start = ((), (), s32[]{:S(2)}) async-start(), calls=%async_computation.25 | async-start | bytes 3276800 | tf_op jit(solution)/shard_map/while/body/eval_jaxpr/reduce_scatter | solution.py:170
  969.3 159.5 %all-gather.20.cloned.1.call-start = ((), (), s32[]{:S(2)}) async-start(), calls=%async_computation.27 | async-start | bytes 1638400 | tf_op jit(solution)/shard_map/while/body/eval_jaxpr/all_gather | solution.py:114
  1139.4 105.2 %reduce-scatter.35.cloned.1.call-start = ((), (), s32[]{:S(2)}) async-start(), calls=%async_computation.25 | async-start | bytes 3276800 | tf_op jit(solution)/shard_map/while/body/eval_jaxpr/reduce_scatter | solution.py:170
  1142.3 159.5 %all-gather.20.cloned.1.call-start = ((), (), s32[]{:S(2)}) async-start(), calls=%async_computation.27 | async-start | bytes 1638400 | tf_op jit(solution)/shard_map/while/body/eval_jaxpr/all_gather | solution.py:114
  1312.3 105.4 %reduce-scatter.35.cloned.1.call-start = ((), (), s32[]{:S(2)}) async-start(), calls=%async_computation.25 | async-start | bytes 3276800 | tf_op jit(solution)/shard_map/while/body/eval_jaxpr/reduce_scatter | solution.py:170
  1315.2 159.6 %all-gather.20.cloned.1.call-start = ((), (), s32[]{:S(2)}) async-start(), calls=%async_computation.27 | async-start | bytes 1638400 | tf_op jit(solution)/shard_map/while/body/eval_jaxpr/all_gather | solution.py:114
  1479.2 57.4 %reduce-scatter.37.cloned.1.call-start = ((), (), s32[]{:S(2)}) async-start(), calls=%async_computation.26 | async-start | bytes 3276800 | tf_op jit(solution)/shard_map/while/body/eval_jaxpr/reduce_scatter | solution.py:107
  1485.3 105.2 %reduce-scatter.35.cloned.1.call-start = ((), (), s32[]{:S(2)}) async-start(), calls=%async_computation.25 | async-start | bytes 3276800 | tf_op jit(solution)/shard_map/while/body/eval_jaxpr/reduce_scatter | solution.py:170
  1488.2 159.5 %all-gather.20.cloned.1.call-start = ((), (), s32[]{:S(2)}) async-start(), calls=%async_computation.27 | async-start | bytes 1638400 | tf_op jit(solution)/shard_map/while/body/eval_jaxpr/all_gather | solution.py:114
  1652.1 57.4 %reduce-scatter.37.cloned.1.call-start = ((), (), s32[]{:S(2)}) async-start(), calls=%async_computation.26 | async-start | bytes 3276800 | tf_op jit(solution)/shard_map/while/body/eval_jaxpr/reduce_scatter | solution.py:107
  1658.2 105.2 %reduce-scatter.35.cloned.1.call-start = ((), (), s32[]{:S(2)}) async-start(), calls=%async_computation.25 | async-start | bytes 3276800 | tf_op jit(solution)/shard_map/while/body/eval_jaxpr/reduce_scatter | solution.py:170
  1661.2 159.5 %all-gather.20.cloned.1.call-start = ((), (), s32[]{:S(2)}) async-start(), calls=%async_computation.27 | async-start | bytes 1638400 | tf_op jit(solution)/shard_map/while/body/eval_jaxpr/all_gather | solution.py:114
  1825.0 57.4 %reduce-scatter.37.cloned.1.call-start = ((), (), s32[]{:S(2)}) async-start(), calls=%async_computation.26 | async-start | bytes 3276800 | tf_op jit(solution)/shard_map/while/body/eval_jaxpr/reduce_scatter | solution.py:107
  1831.1 105.2 %reduce-scatter.35.cloned.1.call-start = ((), (), s32[]{:S(2)}) async-start(), calls=%async_computation.25 | async-start | bytes 3276800 | tf_op jit(solution)/shard_map/while/body/eval_jaxpr/reduce_scatter | solution.py:170
  1834.1 159.5 %all-gather.20.cloned.1.call-start = ((), (), s32[]{:S(2)}) async-start(), calls=%async_computation.27 | async-start | bytes 1638400 | tf_op jit(solution)/shard_map/while/body/eval_jaxpr/all_gather | solution.py:114
  1997.9 57.4 %reduce-scatter.37.cloned.1.call-start = ((), (), s32[]{:S(2)}) async-start(), calls=%async_computation.26 | async-start | bytes 3276800 | tf_op jit(solution)/shard_map/while/body/eval_jaxpr/reduce_scatter | solution.py:107
  2004.1 105.2 %reduce-scatter.35.cloned.1.call-start = ((), (), s32[]{:S(2)}) async-start(), calls=%async_computation.25 | async-start | bytes 3276800 | tf_op jit(solution)/shard_map/while/body/eval_jaxpr/reduce_scatter | solution.py:170
  2007.0 159.5 %all-gather.20.cloned.1.call-start = ((), (), s32[]{:S(2)}) async-start(), calls=%async_computation.27 | async-start | bytes 1638400 | tf_op jit(solution)/shard_map/while/body/eval_jaxpr/all_gather | solution.py:114
  2170.8 57.4 %reduce-scatter.37.cloned.1.call-start = ((), (), s32[]{:S(2)}) async-start(), calls=%async_computation.26 | async-start | bytes 3276800 | tf_op jit(solution)/shard_map/while/body/eval_jaxpr/reduce_scatter | solution.py:107
  2177.0 105.2 %reduce-scatter.35.cloned.1.call-start = ((), (), s32[]{:S(2)}) async-start(), calls=%async_computation.25 | async-start | bytes 3276800 | tf_op jit(solution)/shard_map/while/body/eval_jaxpr/reduce_scatter | solution.py:170
  2179.9 159.5 %all-gather.20.cloned.1.call-start = ((), (), s32[]{:S(2)}) async-start(), calls=%async_computation.27 | async-start | bytes 1638400 | tf_op jit(solution)/shard_map/while/body/eval_jaxpr/all_gather | solution.py:114
  2343.7 57.4 %reduce-scatter.37.cloned.1.call-start = ((), (), s32[]{:S(2)}) async-start(), calls=%async_computation.26 | async-start | bytes 3276800 | tf_op jit(solution)/shard_map/while/body/eval_jaxpr/reduce_scatter | solution.py:107
  2349.9 105.2 %reduce-scatter.35.cloned.1.call-start = ((), (), s32[]{:S(2)}) async-start(), calls=%async_computation.25 | async-start | bytes 3276800 | tf_op jit(solution)/shard_map/while/body/eval_jaxpr/reduce_scatter | solution.py:170
  2352.8 159.5 %all-gather.20.cloned.1.call-start = ((), (), s32[]{:S(2)}) async-start(), calls=%async_computation.27 | async-start | bytes 1638400 | tf_op jit(solution)/shard_map/while/body/eval_jaxpr/all_gather | solution.py:114
  2519.2 57.4 %reduce-scatter.33.cloned.1.call-start = ((), (), s32[]{:S(2)}) async-start(), calls=%async_computation.23 | async-start | bytes 3276800 | tf_op jit(solution)/shard_map/while/body/eval_jaxpr/reduce_scatter | solution.py:107
  2525.4 87.0 %all-gather.18.cloned.1.call-start = ((), (), s32[]{:S(2)}) async-start(), calls=%async_computation.24 | async-start | bytes 1638400 | tf_op jit(solution)/shard_map/while/body/eval_jaxpr/all_gather | solution.py:114
  2621.1 87.0 %all-gather.18.cloned.1.call-start = ((), (), s32[]{:S(2)}) async-start(), calls=%async_computation.24 | async-start | bytes 1638400 | tf_op jit(solution)/shard_map/while/body/eval_jaxpr/all_gather | solution.py:114
  2710.6 57.4 %reduce-scatter.33.cloned.1.call-start = ((), (), s32[]{:S(2)}) async-start(), calls=%async_computation.23 | async-start | bytes 3276800 | tf_op jit(solution)/shard_map/while/body/eval_jaxpr/reduce_scatter | solution.py:107
  2716.8 87.0 %all-gather.18.cloned.1.call-start = ((), (), s32[]{:S(2)}) async-start(), calls=%async_computation.24 | async-start | bytes 1638400 | tf_op jit(solution)/shard_map/while/body/eval_jaxpr/all_gather | solution.py:114
  2806.3 57.4 %reduce-scatter.33.cloned.1.call-start = ((), (), s32[]{:S(2)}) async-start(), calls=%async_computation.23 | async-start | bytes 3276800 | tf_op jit(solution)/shard_map/while/body/eval_jaxpr/reduce_scatter | solution.py:107
  2812.5 87.0 %all-gather.18.cloned.1.call-start = ((), (), s32[]{:S(2)}) async-start(), calls=%async_computation.24 | async-start | bytes 1638400 | tf_op jit(solution)/shard_map/while/body/eval_jaxpr/all_gather | solution.py:114
  2902.0 57.4 %reduce-scatter.33.cloned.1.call-start = ((), (), s32[]{:S(2)}) async-start(), calls=%async_computation.23 | async-start | bytes 3276800 | tf_op jit(solution)/shard_map/while/body/eval_jaxpr/reduce_scatter | solution.py:107
  2908.2 87.0 %all-gather.18.cloned.1.call-start = ((), (), s32[]{:S(2)}) async-start(), calls=%async_computation.24 | async-start | bytes 1638400 | tf_op jit(solution)/shard_map/while/body/eval_jaxpr/all_gather | solution.py:114
  3003.8 87.0 %all-gather.18.cloned.1.call-start = ((), (), s32[]{:S(2)}) async-start(), calls=%async_computation.24 | async-start | bytes 1638400 | tf_op jit(solution)/shard_map/while/body/eval_jaxpr/all_gather | solution.py:114
  3099.5 87.0 %all-gather.18.cloned.1.call-start = ((), (), s32[]{:S(2)}) async-start(), calls=%async_computation.24 | async-start | bytes 1638400 | tf_op jit(solution)/shard_map/while/body/eval_jaxpr/all_gather | solution.py:114
  3195.2 87.0 %all-gather.18.cloned.1.call-start = ((), (), s32[]{:S(2)}) async-start(), calls=%async_computation.24 | async-start | bytes 1638400 | tf_op jit(solution)/shard_map/while/body/eval_jaxpr/all_gather | solution.py:114
  3290.9 87.0 %all-gather.18.cloned.1.call-start = ((), (), s32[]{:S(2)}) async-start(), calls=%async_computation.24 | async-start | bytes 1638400 | tf_op jit(solution)/shard_map/while/body/eval_jaxpr/all_gather | solution.py:114
  3386.6 87.0 %all-gather.18.cloned.1.call-start = ((), (), s32[]{:S(2)}) async-start(), calls=%async_computation.24 | async-start | bytes 1638400 | tf_op jit(solution)/shard_map/while/body/eval_jaxpr/all_gather | solution.py:114
  3482.3 87.0 %all-gather.18.cloned.1.call-start = ((), (), s32[]{:S(2)}) async-start(), calls=%async_computation.24 | async-start | bytes 1638400 | tf_op jit(solution)/shard_map/while/body/eval_jaxpr/all_gather | solution.py:114
  3571.8 57.4 %reduce-scatter.33.cloned.1.call-start = ((), (), s32[]{:S(2)}) async-start(), calls=%async_computation.23 | async-start | bytes 3276800 | tf_op jit(solution)/shard_map/while/body/eval_jaxpr/reduce_scatter | solution.py:107
  3578.0 87.0 %all-gather.18.cloned.1.call-start = ((), (), s32[]{:S(2)}) async-start(), calls=%async_computation.24 | async-start | bytes 1638400 | tf_op jit(solution)/shard_map/while/body/eval_jaxpr/all_gather | solution.py:114
  3667.5 77.9 %all-gather.16.cloned.1.call-start = ((), (), s32[]{:S(2)}) async-start(), calls=%async_computation.15 | async-start | bytes 4915200 | tf_op jit(solution)/shard_map/all_gather | solution.py:198
  3668.2 120.7 %all-gather.14.cloned.1.call-start = ((), (), s32[]{:S(2)}) async-start(), calls=%async_computation.14 | async-start | bytes 2457600 | tf_op jit(solution)/shard_map/all_gather | solution.py:161
  3670.2 535.6 %all-reduce.2.cloned.1.call-start = ((), (), s32[]{:S(2)}) async-start(), calls=%async_computation.16 | async-start | bytes 3932160 | tf_op jit(solution)/shard_map/psum | solution.py:217
  4124.8 117.7 %reduce-scatter.31.cloned.1.call-start = ((), (), s32[]{:S(2)}) async-start(), calls=%async_computation.22 | async-start | bytes 737280
  4128.1 155.6 %reduce-scatter.29.cloned.1.call-start = ((), (), s32[]{:S(2)}) async-start(), calls=%async_computation.21 | async-start | bytes 1474560
  4138.2 182.2 %reduce-scatter.27.cloned.1.call-start = ((), (), s32[]{:S(2)}) async-start(), calls=%async_computation.20 | async-start | bytes 368640
  4212.8 144.4 %reduce-scatter.25.cloned.1.call-start = ((), (), s32[]{:S(2)}) async-start(), calls=%async_computation.19 | async-start | bytes 368640
  4213.8 194.1 %reduce-scatter.21.cloned.1.call-start = ((), (), s32[]{:S(2)}) async-start(), calls=%async_computation.17 | async-start | bytes 3686400 | tf_op jit(solution)/shard_map/reduce_scatter | solution.py:200
  4214.4 244.3 %reduce-scatter.23.cloned.1.call-start = ((), (), s32[]{:S(2)}) async-start(), calls=%async_computation.18 | async-start | bytes 3686400 | tf_op jit(solution)/shard_map/reduce_scatter | solution.py:201
  (147 other events, 3119.0 us)
Sparse Core Ops, SparseCore 0:
  233.5 72.9 reduce-scatter.18
  309.2 76.8 all-gather.7
  446.6 52.0 reduce-scatter.36
  500.9 51.7 reduce-scatter.34
  575.7 34.1 all-gather.19
  620.5 51.0 reduce-scatter.36
  674.0 51.7 reduce-scatter.34
  748.8 34.0 all-gather.19
  793.6 51.1 reduce-scatter.36
  846.9 51.7 reduce-scatter.34
  921.8 34.0 all-gather.19
  966.5 51.0 reduce-scatter.36
  1019.8 51.7 reduce-scatter.34
  1094.7 34.1 all-gather.19
  1139.5 51.0 reduce-scatter.36
  1192.8 51.7 reduce-scatter.34
  1267.6 34.1 all-gather.19
  1312.4 51.0 reduce-scatter.36
  1365.8 51.7 reduce-scatter.34
  1440.6 34.1 all-gather.19
  1485.4 51.0 reduce-scatter.36
  1538.7 51.7 reduce-scatter.34
  1613.6 34.0 all-gather.19
  1658.4 51.1 reduce-scatter.36
  1711.7 51.7 reduce-scatter.34
  1786.5 34.0 all-gather.19
  1831.3 51.0 reduce-scatter.36
  1884.5 51.7 reduce-scatter.34
  1959.4 34.1 all-gather.19
  2004.2 51.0 reduce-scatter.36
  2057.5 51.7 reduce-scatter.34
  2132.4 34.0 all-gather.19
  2177.1 51.1 reduce-scatter.36
  2230.4 51.7 reduce-scatter.34
  2305.3 34.0 all-gather.19
  2350.0 51.0 reduce-scatter.36
  2403.3 51.7 reduce-scatter.34
  2478.2 34.0 all-gather.19
  2525.5 51.0 reduce-scatter.32
  2621.2 51.0 reduce-scatter.32
  2675.7 32.3 all-gather.17
  2716.9 51.0 reduce-scatter.32
  2771.4 32.3 all-gather.17
  2812.6 51.0 reduce-scatter.32
  2908.3 51.0 reduce-scatter.32
  3004.0 51.0 reduce-scatter.32
  3099.6 51.0 reduce-scatter.32
  3195.3 51.0 reduce-scatter.32
  3249.8 32.3 all-gather.17
  3291.0 51.0 reduce-scatter.32
  3386.7 51.0 reduce-scatter.32
  3482.4 51.0 reduce-scatter.32
  3536.9 32.3 all-gather.17
  3578.1 51.0 reduce-scatter.32
  3632.6 32.3 all-gather.17
  3669.9 75.4 all-gather.15
  3746.8 42.1 all-gather.13
  4124.9 80.7 all-reduce.1
  4208.8 33.5 reduce-scatter.30
  4246.3 37.3 reduce-scatter.28
  4286.6 33.7 reduce-scatter.26
  4323.4 33.7 reduce-scatter.24
  4361.0 46.8 reduce-scatter.20
  4411.8 46.8 reduce-scatter.22
  (9 shorter events, 276.7 us)
